TPU v7x, 32 devices: a whole 2x2x4 slice. The times are simulated.
32 devices in a mesh: ctx: 8 (over z, core), tp: 4 (over y, x).
Axes of the slice: x: 2, y: 2, z: 4, core: 2. Of those that a mesh axis runs over, the one named last changes fastest.
Arguments:
- hidden_rows: bfloat16 [4096, 8192], P('ctx', 'tp'), may hold values from -6 to 6
- w_value: bfloat16 [8192, 8192], P('ctx', 'tp'), may hold values from -0.0625 to 0.0625
- w_gate: bfloat16 [8192, 8192], P('ctx', 'tp'), may hold values from -0.0625 to 0.0625
- state_proj: bfloat16 [4096, 2, 4, 256], P('ctx'), may hold values from -1.5 to 1.5
- rates: float32 [4096, 128], P('ctx', 'tp'), may hold values from 0 to 4.5, as said below
- read_weights: float32 [6, 4096, 128], P(None, 'ctx', 'tp'), may hold values from 0.25 to 2
- prior_state: float32 [128, 64, 256], P('tp'), may hold values from -24 to 24
- skip_weight: float32 [128], P('tp'), may hold values from 0.5 to 2
- norm_gain: float32 [8192], P('tp'), may hold values from 0.25 to 1.75
Outputs:
- layer_out: bfloat16 [4096, 8192], P('ctx', 'tp')
Inputs may be any that keep to these rules, and one draw needn't show every extreme that they name: Positive rates.
All inputs are finite; a program needn't handle non-finite values.
Results may differ from a plain program's by a relative error of at most 0.0085.
Values may be sent and summed in bfloat16 or wider, within the bound.
A program may use at most 128 MiB of HBM per device.

v0:
```python
import jax
import jax.numpy as jnp
from jax import lax
from jax.sharding import PartitionSpec as P

HEAD_DIM = 64
STATE = 256
HPG = 32
LEVELS = 6


def swapped(value, axis, distance):
    return lax.ppermute(value, axis, [(i, i ^ 1 << distance) for i in range(lax.axis_size(axis))])


def on_device(
    hidden_rows,
    w_value,
    w_gate,
    state_proj,
    rates,
    read_weights,
    prior_state,
    skip_weight,
    norm_gain,
):
    tok_rows = rates.shape[0]
    head_count = rates.shape[1]
    level_total = LEVELS - 2
    full_rows = lax.all_gather(hidden_rows, "tp", axis=1, tiled=True)
    value_sum = jnp.dot(
        full_rows,
        lax.all_gather(w_value, "ctx", axis=0, tiled=True),
        preferred_element_type=jnp.float32,
    )
    gate_sum = jnp.dot(
        full_rows,
        lax.all_gather(w_gate, "ctx", axis=0, tiled=True),
        preferred_element_type=jnp.float32,
    )
    values_proj = value_sum.astype(jnp.bfloat16)
    gates_proj = gate_sum.astype(jnp.bfloat16)
    values3 = values_proj.reshape(tok_rows, head_count, HEAD_DIM)
    group_index = lax.axis_index("tp") * head_count // HPG
    write_vec = lax.dynamic_index_in_dim(state_proj[:, 0], group_index, 1, keepdims=False)
    read_vec = lax.dynamic_index_in_dim(state_proj[:, 1], group_index, 1, keepdims=False)
    cum_rate = jnp.cumsum(rates, axis=0)
    scores = lax.dot_general(
        read_vec, write_vec, (((1,), (1,)), ((), ())), preferred_element_type=jnp.float32
    )
    rate_lag = cum_rate.T[:, :, None] - cum_rate.T[:, None, :]
    causal = (jnp.arange(tok_rows)[:, None] >= jnp.arange(tok_rows)[None, :])[None]
    mixing = (
        jnp.where(causal, jnp.exp(-jnp.where(causal, rate_lag, 0.0)), 0.0) * scores[None]
    ).astype(jnp.bfloat16)
    local_out = jnp.einsum("hts,shp->thp", mixing, values3, preferred_element_type=jnp.float32)
    span_total = cum_rate[-1]
    write_weighted = (
        jnp.exp(-(span_total[None] - cum_rate))[:, :, None]
        * write_vec[:, None, :].astype(jnp.float32)
    ).astype(jnp.bfloat16)
    end_state = jnp.einsum(
        "thn,thp->hpn", write_weighted, values3, preferred_element_type=jnp.float32
    )
    my_block = lax.axis_index("ctx")
    agg_state = end_state
    agg_rate = span_total
    start_rate = jnp.zeros((head_count,), jnp.float32)
    tier_components = []
    for bit_pos in range(lax.axis_size("ctx").bit_length() - 1):
        other_state, other_rate = swapped((agg_state, agg_rate), "ctx", bit_pos)
        is_upper = jnp.right_shift(my_block, bit_pos) % 2 == 1
        tier_components.append(
            jnp.where(is_upper, other_state * jnp.exp(-start_rate)[:, None, None], 0.0)
        )
        agg_state = jnp.where(
            is_upper,
            other_state * jnp.exp(-agg_rate)[:, None, None] + agg_state,
            agg_state * jnp.exp(-other_rate)[:, None, None] + other_state,
        )
        agg_rate = agg_rate + other_rate
        start_rate = jnp.where(is_upper, start_rate + other_rate, start_rate)
    for extra_level in range(level_total - len(tier_components)):
        tier_components.append(jnp.zeros((head_count, HEAD_DIM, STATE), jnp.float32))
    carried = jnp.stack(tier_components)
    prior_part = jnp.exp(-start_rate)[:, None, None] * prior_state
    states = jnp.concatenate([carried, prior_part[None]], axis=0)
    projected = jnp.einsum(
        "tn,lhpn->tlhp", read_vec.astype(jnp.float32), states, precision=lax.Precision.HIGHEST
    )
    read_scale = read_weights[1:] * jnp.exp(-cum_rate)[None]
    carried_out = jnp.einsum(
        "lth,tlhp->thp", read_scale, projected, precision=lax.Precision.HIGHEST
    )
    mixed_out = (
        read_weights[0][:, :, None] * local_out
        + carried_out
        + skip_weight[None, :, None] * values3.astype(jnp.float32)
    )
    gates3 = gates_proj.reshape(tok_rows, head_count, HEAD_DIM).astype(jnp.float32)
    filtered_result = mixed_out * jax.nn.silu(gates3)
    inverse = lax.rsqrt(jnp.mean(filtered_result * filtered_result, axis=2, keepdims=True) + 1e-05)
    result = filtered_result * inverse * norm_gain.reshape(head_count, HEAD_DIM)[None]
    return result.reshape(tok_rows, head_count * HEAD_DIM).astype(jnp.bfloat16)


def solution(mesh):
    in_specs = (
        P("ctx", "tp"),
        P("ctx", "tp"),
        P("ctx", "tp"),
        P("ctx", None, None, None),
        P("ctx", "tp"),
        P(None, "ctx", "tp"),
        P("tp", None, None),
        P("tp"),
        P("tp"),
    )
    out_specs = P("ctx", "tp")
    return jax.shard_map(
        on_device, mesh=mesh, in_specs=in_specs, out_specs=out_specs, check_vma=False
    )
```

profile of v0, /device:TPU:17, one launch (start us, length us, event | category | flops | bytes accessed | tf_op | source)
XLA Modules:
  0.0 836.5 jit_solution(6695829626215990275)
XLA Ops:
  6.5 0.7 all-gather.4.cloned.1.call-update
  7.3 0.0 copy-start.4
  7.3 0.0 all-gather.6.cloned.1.call-start
  7.3 0.7 all-gather.6.cloned.1.call-update
  8.0 0.0 all-gather.8.cloned.1.call-start
  8.1 0.7 all-gather.8.cloned.1.call-update
  8.8 1.2 reduce-window.6
  10.0 0.2 slice_reduce_fusion
  10.2 0.7 copy_bitcast_fusion.2
  10.9 0.2 slice_reduce_fusion.1
  11.1 0.7 fusion.19
  11.8 1.1 constant_dynamic-slice_fusion
  12.9 0.7 negate_exponential_fusion
  13.6 0.9 fusion.12
  14.5 83.1 %all-gather.4.cloned.1.call-done = bf16[512,8192]{1,0:T(8,128)(2,1)} async-done(((bf16[512,2048]{1,0:T(8,128)(2,1)}), bf16[512,8192]{1,0:T(8,128)(2,1)}) %all-gather.4.cloned.1.call-update) | async-done | bytes 8388624 | tf_op jit(solution)/shard_map/all_gather | solution.py:30
  97.6 289.0 %all-gather.6.cloned.1.call-done = bf16[8192,2048]{1,0:T(8,128)(2,1)} async-done(((bf16[1024,2048]{1,0:T(8,128)(2,1)}), bf16[8192,2048]{1,0:T(8,128)(2,1)}) %all-gather.6.cloned.1.call-update) | async-done | bytes 33554448 | tf_op jit(solution)/shard_map/all_gather | solution.py:33
  386.6 25.6 %convolution_convert_fusion.1 = bf16[512,2048]{1,0:T(8,128)(2,1)} fusion(bf16[512,8192]{1,0:T(8,128)(2,1)} %all-gather.4.cloned.1.call-done, bf16[8192,2048]{1,0:T(8,128)(2,1)} %all-gather.6.cloned.1.call-done), kind=kOutput, calls=%fused_computation.16 | convolution fusion | flops 17180917760 | bytes 44040192 | tf_op jit(solution)/shard_map/dot_general | solution.py:31
  412.2 2.9 copy.27
  415.1 0.0 copy-start.6
  415.1 1.3 copy-done.6
  416.4 5.1 fusion.2
  421.5 0.3 collective-permute-start
  421.8 0.2 collective-permute-start.1
  422.0 3.9 collective-permute-done.1
  425.9 0.5 negate_exponential_fusion.4
  426.4 0.0 collective-permute-start.3
  426.4 3.0 collective-permute-done.3
  429.4 0.6 add.71
  430.0 1.7 collective-permute-start.5
  431.7 0.0 copy-done.16
  431.7 2.3 collective-permute-done.5
  434.0 1.2 fusion.16
  435.3 0.0 collective-permute-done
  435.3 1.3 copy-done.2
  436.6 3.4 add_select_fusion.1
  440.0 2.6 collective-permute-start.2
  442.6 0.8 mul.166
  443.4 0.8 iota_compare_fusion
  444.1 0.0 copy-done.9
  444.1 0.6 slice_bitcast_fusion
  444.8 1.6 multiply_bitcast_fusion
  446.4 1.3 fusion.10
  447.7 0.7 negate_exponential_fusion.2
  448.3 188.4 %collective-permute-done.2 = f32[32,64,256]{2,1,0:T(8,128)S(1)} collective-permute-done((f32[32,64,256]{2,1,0:T(8,128)}, f32[32,64,256]{2,1,0:T(8,128)S(1)}, u32[]{:S(2)}, u32[]{:S(2)}) %collective-permute-start.2) | collective-permute-done | bytes 2097184 | tf_op jit(solution)/shard_map/ppermute | solution.py:13
  636.8 3.4 add_select_fusion
  640.1 4.6 collective-permute-start.4
  644.7 120.0 %all-gather.8.cloned.1.call-done = bf16[8192,2048]{1,0:T(8,128)(2,1)} async-done(((bf16[1024,2048]{1,0:T(8,128)(2,1)}), bf16[8192,2048]{1,0:T(8,128)(2,1)}) %all-gather.8.cloned.1.call-update) | async-done | bytes 33554448 | tf_op jit(solution)/shard_map/all_gather | solution.py:38
  764.8 24.8 %fusion.8 = f32[512,2048]{1,0:T(8,128)} fusion(bf16[512,8192]{1,0:T(8,128)(2,1)} %all-gather.4.cloned.1.call-done, bf16[8192,2048]{1,0:T(8,128)(2,1)} %all-gather.8.cloned.1.call-done), kind=kOutput, calls=%fused_computation.15 | convolution fusion | flops 17181966336 | bytes 46137344 | tf_op jit(solution)/shard_map/dot_general | solution.py:36
  789.5 5.3 copy.32
  794.9 1.8 bitcast_dynamic-update-slice_fusion.3
  796.7 0.2 bitcast_dynamic-update-slice_fusion.2
  796.9 0.0 copy-start.5
  796.9 0.0 collective-permute-done.4
  796.9 1.9 bitcast_dynamic-update-slice_fusion.1
  798.9 0.1 broadcast_dynamic-update-slice_fusion
  799.0 0.1 copy-done.5
  799.1 0.2 bitcast_dynamic-update-slice_fusion
  799.3 0.6 copy-done.10
  799.9 0.0 copy-start.17
  800.0 13.2 %multiply_reduce_fusion = f32[512,32,64]{0,2,1:T(8,128)} fusion(f32[512,32,5]{0,1,2:T(8,128)S(1)} %copy-done.10, f32[5,32,64,256]{3,2,1,0:T(8,128)S(1)} %bitcast_dynamic-update-slice_fusion, bf16[512,1,1,256]{3,2,1,0:T(2,128)(2,1)S(1)} %get-tuple-element.22), kind=kOutput, calls=%fused_computation.1 | convolution fusion | flops 16115564544 | bytes 15269888 | tf_op jit(solution)/shard_map/tn,lhpn->tlhp/dot_general | solution.py:88
  813.2 13.6 %multiply_reduce_fusion.1 = (f32[512,32]{0,1:T(8,128)S(1)}, f32[512,32,64]{0,2,1:T(8,128)S(1)}) fusion(f32[512,32,64]{0,2,1:T(8,128)S(1)} %bitcast.69, bf16[512,32,64]{0,2,1:T(8,128)(2,1)S(1)} %bitcast.71, f32[32]{0:T(128)S(1)} %copy-done.17, f32[512,32,64]{0,2,1:T(8,128)} %multiply_reduce_fusion, f32[512,512]{1,0:T(8,128)S(1)} %copy-done.8, ...), kind=kOutput, calls=%fused_computation.13 | convolution fusion | flops 1136640000 | bytes 16187520 | tf_op jit(solution)/shard_map/hts,shp->thp/dot_general | solution.py:56
  826.8 0.0 copy-start.1
  826.8 0.7 multiply_convert_fusion.4
  827.5 2.4 copy.33
  (30 shorter events, 0.1 us)
Async XLA Ops:
  6.5 2.2 copy-start
  6.5 91.1 %all-gather.4.cloned.1.call-start = ((), (), s32[]{:S(2)}) async-start(), calls=%async_computation | async-start | bytes 10485760 | tf_op jit(solution)/shard_map/all_gather | solution.py:30
  7.3 3.8 copy-start.4
  7.3 379.3 %all-gather.6.cloned.1.call-start = ((), (), s32[]{:S(2)}) async-start(), calls=%async_computation.1 | async-start | bytes 37748736 | tf_op jit(solution)/shard_map/all_gather | solution.py:33
  8.0 756.7 %all-gather.8.cloned.1.call-start = ((), (), s32[]{:S(2)}) async-start(), calls=%async_computation.2 | async-start | bytes 37748736 | tf_op jit(solution)/shard_map/all_gather | solution.py:38
  415.1 1.3 copy-start.6
  421.5 22.6 %copy-start.9 = (f32[6,512,32]{1,2,0:T(8,128)S(1)}, f32[6,512,32]{1,2,0:T(8,128)}, u32[]{:S(2)}) copy-start(f32[6,512,32]{1,2,0:T(8,128)} %param.14) | copy-start | bytes 1179652
  421.5 13.8 %collective-permute-start = (f32[32,64,256]{2,1,0:T(8,128)}, f32[32,64,256]{2,1,0:T(8,128)S(1)}, u32[]{:S(2)}, u32[]{:S(2)}) collective-permute-start(f32[32,64,256]{2,1,0:T(8,128)} %fusion.2), channel_id=1, source_target_pairs={{0,4},{4,0},{8,12},{12,8},{16,20},{20,16},{24,28},{28,24},{1,5},{5... | collective-permute-start | bytes 6291464 | tf_op jit(solution)/shard_map/ppermute | solution.py:13
  421.8 4.1 collective-permute-start.1
  426.4 3.0 collective-permute-start.3
  429.4 2.3 copy-start.16
  430.0 4.1 collective-permute-start.5
  435.3 1.3 copy-start.2
  440.0 196.8 %collective-permute-start.2 = (f32[32,64,256]{2,1,0:T(8,128)}, f32[32,64,256]{2,1,0:T(8,128)S(1)}, u32[]{:S(2)}, u32[]{:S(2)}) collective-permute-start(f32[32,64,256]{2,1,0:T(8,128)} %add_select_fusion.1), channel_id=1, source_target_pairs={{0,8},{4,12},{8,0},{12,4},{16,24},{20,28},{24,16},{28,20},{1,9},{5... | collective-permute-start | bytes 6291464 | tf_op jit(solution)/shard_map/ppermute | solution.py:13
  640.1 156.8 %collective-permute-start.4 = (f32[32,64,256]{2,1,0:T(8,128)}, f32[32,64,256]{2,1,0:T(8,128)}, u32[]{:S(2)}, u32[]{:S(2)}) collective-permute-start(f32[32,64,256]{2,1,0:T(8,128)} %add_select_fusion), channel_id=1, source_target_pairs={{0,16},{4,20},{8,24},{12,28},{16,0},{20,4},{24,8},{28,12},{1,17},{... | collective-permute-start | bytes 6291464 | tf_op jit(solution)/shard_map/ppermute | solution.py:13
  794.9 1.8 copy-start.15
  796.9 2.2 copy-start.5
  796.9 2.2 copy-start.14
  798.9 1.0 copy-start.10
  799.9 13.2 %copy-start.3 = (f32[512,2048]{0,1:T(8,128)S(1)}, f32[512,2048]{0,1:T(8,128)}, u32[]{:S(2)}) copy-start(f32[512,2048]{0,1:T(8,128)} %copy.32) | copy-start | bytes 12582916
  799.9 13.2 %copy-start.7 = (bf16[512,2048]{0,1:T(8,128)(2,1)S(1)}, bf16[512,2048]{0,1:T(8,128)(2,1)}, u32[]{:S(2)}) copy-start(bf16[512,2048]{0,1:T(8,128)(2,1)} %copy-done.6) | copy-start | bytes 6291460
  799.9 13.2 %copy-start.8 = (f32[512,512]{1,0:T(8,128)S(1)}, f32[512,512]{1,0:T(8,128)}, u32[]{:S(2)}) copy-start(f32[512,512]{1,0:T(8,128)} %fusion.10) | copy-start | bytes 3145732
  799.9 13.2 %copy-start.11 = (pred[512,512]{1,0:T(8,128)(4,1)S(1)}, pred[512,512]{1,0:T(8,128)(4,1)}, u32[]{:S(2)}) copy-start(pred[512,512]{1,0:T(8,128)(4,1)} %iota_compare_fusion) | copy-start | bytes 786436
  799.9 13.2 %copy-start.12 = (f32[32,512]{1,0:T(8,128)S(1)}, f32[32,512]{1,0:T(8,128)}, u32[]{:S(2)}) copy-start(f32[32,512]{1,0:T(8,128)} %get-tuple-element.11) | copy-start | bytes 196612
  799.9 13.2 %copy-start.13 = (f32[512,32]{0,1:T(8,128)S(1)}, f32[512,32]{0,1:T(8,128)}, u32[]{:S(2)}) copy-start(f32[512,32]{0,1:T(8,128)} %slice_bitcast_fusion) | copy-start | bytes 196612
  799.9 13.2 %copy-start.17 = (f32[32]{0:T(128)S(1)}, f32[32]{0:T(128)}, u32[]{:S(2)}) copy-start(f32[32]{0:T(128)} %param.16) | copy-start | bytes 388
  826.8 3.1 copy-start.1
Sparse Core Ops, SparseCore 0:
  9.2 88.3 all-gather.3
  99.2 287.3 all-gather.5
  388.2 376.4 all-gather.7
where the time goes:
time: 837 us; the launch traced here: 836 us
  waiting for transfers between devices  692 us (83%)
  matrix products  83.6 us (10%)
  other arithmetic  20.6 us (2%)
  local copies, waits for them, and re-layouts  17.6 us (2%)
  between operations  13.4 us (2%)
  starting transfers between devices  9.53 us (1%)
    all_gather x1, waiting for transfers between devices, on_device(): lax.all_gather(w_value, 'ctx', axis=0, tiled=True)  289 us
    ppermute x6, waiting for transfers between devices, swapped(): lax.ppermute(value, axis, [(i, i ^ 1 << distance) for i in range(lax.axis...  198 us
    all_gather x1, waiting for transfers between devices, on_device(): lax.all_gather(w_gate, 'ctx', axis=0, tiled=True)  120 us
    all_gather x1, waiting for transfers between devices, on_device(): full_rows = lax.all_gather(hidden_rows, 'tp', axis=1, tiled=True)  83.1 us
    dot_general x1, matrix products, on_device(): jnp.dot(full_rows, lax.all_gather(w_value, 'ctx', axis=0, tiled=True), pr...  25.6 us
    dot_general x1, matrix products, on_device(): jnp.dot(full_rows, lax.all_gather(w_gate, 'ctx', axis=0, tiled=True), pre...  24.8 us
  transfers between devices with their start and end apart: 9, of which 7 were waited for; matrix products, arithmetic and copies ran while one was open for 10% of the time, Pallas kernels for 0%

commit v1 on v0

--- a/solution.py
+++ b/solution.py
@@ -27,19 +27,29 @@
     tok_rows = rates.shape[0]
     head_count = rates.shape[1]
     level_total = LEVELS - 2
-    full_rows = lax.all_gather(hidden_rows, "tp", axis=1, tiled=True)
-    value_sum = jnp.dot(
-        full_rows,
-        lax.all_gather(w_value, "ctx", axis=0, tiled=True),
-        preferred_element_type=jnp.float32,
-    )
-    gate_sum = jnp.dot(
-        full_rows,
-        lax.all_gather(w_gate, "ctx", axis=0, tiled=True),
-        preferred_element_type=jnp.float32,
-    )
-    values_proj = value_sum.astype(jnp.bfloat16)
-    gates_proj = gate_sum.astype(jnp.bfloat16)
+    ctx_size = lax.axis_size("ctx")
+    half = ctx_size // 2
+    my_block = lax.axis_index("ctx")
+    upper_half = my_block // half
+    groups = [list(range(half)), list(range(half, ctx_size))]
+    across = [(i, (i + half) % ctx_size) for i in range(ctx_size)]
+    w_value_half = lax.all_gather(w_value, "ctx", axis=0, tiled=True, axis_index_groups=groups)
+    token_part = lax.all_to_all(hidden_rows, "tp", 0, 1, tiled=True)
+    depth = token_part.shape[1] // 2
+    kept = lax.dynamic_slice_in_dim(token_part, upper_half * depth, depth, 1)
+    given = lax.dynamic_slice_in_dim(token_part, (1 - upper_half) * depth, depth, 1)
+    taken = lax.ppermute(given, "ctx", across)
+    rows = lax.all_gather(jnp.stack([kept, taken]), "tp", axis=1, tiled=True)
+    w_gate_half = lax.all_gather(w_gate, "ctx", axis=0, tiled=True, axis_index_groups=groups)
+
+    def project(weight):
+        other = jnp.dot(rows[1], weight, preferred_element_type=jnp.float32).astype(jnp.bfloat16)
+        back = lax.ppermute(other, "ctx", across)
+        mine = jnp.dot(rows[0], weight, preferred_element_type=jnp.float32)
+        return (mine + back.astype(jnp.float32)).astype(jnp.bfloat16)
+
+    values_proj = project(w_value_half)
+    gates_proj = project(w_gate_half)
     values3 = values_proj.reshape(tok_rows, head_count, HEAD_DIM)
     group_index = lax.axis_index("tp") * head_count // HPG
     write_vec = lax.dynamic_index_in_dim(state_proj[:, 0], group_index, 1, keepdims=False)
@@ -62,36 +72,43 @@
     end_state = jnp.einsum(
         "thn,thp->hpn", write_weighted, values3, preferred_element_type=jnp.float32
     )
-    my_block = lax.axis_index("ctx")
     agg_state = end_state
     agg_rate = span_total
     start_rate = jnp.zeros((head_count,), jnp.float32)
     tier_components = []
-    for bit_pos in range(lax.axis_size("ctx").bit_length() - 1):
-        other_state, other_rate = swapped((agg_state, agg_rate), "ctx", bit_pos)
+    bits = ctx_size.bit_length() - 1
+    for bit_pos in range(bits):
         is_upper = jnp.right_shift(my_block, bit_pos) % 2 == 1
+        if bit_pos < bits - 1:
+            other_state, other_rate = swapped((agg_state.astype(jnp.bfloat16), agg_rate), "ctx", bit_pos)
+        else:
+            share = head_count // half
+            piece = lax.dynamic_slice_in_dim(
+                agg_state.astype(jnp.bfloat16), (my_block % half) * share, share, 0
+            )
+            piece, other_rate = swapped((piece, agg_rate), "ctx", bit_pos)
+            other_state = lax.all_gather(piece, "ctx", axis=0, tiled=True, axis_index_groups=groups)
+        other_state = other_state.astype(jnp.float32)
         tier_components.append(
-            jnp.where(is_upper, other_state * jnp.exp(-start_rate)[:, None, None], 0.0)
+            jnp.where(is_upper, other_state * jnp.exp(-start_rate)[:, None, None], 0.0).astype(jnp.bfloat16)
         )
-        agg_state = jnp.where(
-            is_upper,
-            other_state * jnp.exp(-agg_rate)[:, None, None] + agg_state,
-            agg_state * jnp.exp(-other_rate)[:, None, None] + other_state,
+        if bit_pos < bits - 1:
+            agg_state = jnp.where(
+                is_upper,
+                other_state * jnp.exp(-agg_rate)[:, None, None] + agg_state,
+                agg_state * jnp.exp(-other_rate)[:, None, None] + other_state,
+            )
+            agg_rate = agg_rate + other_rate
+        start_rate = jnp.where(is_upper, start_rate + other_rate, start_rate)
+    level_ids = list(range(1, 1 + len(tier_components))) + [level_total + 1]
+    prior_part = (jnp.exp(-start_rate)[:, None, None] * prior_state).astype(jnp.bfloat16)
+    carried_out = 0.0
+    for level, state in zip(level_ids, tier_components + [prior_part]):
+        projected = lax.dot_general(
+            read_vec, state, (((1,), (2,)), ((), ())), preferred_element_type=jnp.float32
         )
-        agg_rate = agg_rate + other_rate
-        start_rate = jnp.where(is_upper, start_rate + other_rate, start_rate)
-    for extra_level in range(level_total - len(tier_components)):
-        tier_components.append(jnp.zeros((head_count, HEAD_DIM, STATE), jnp.float32))
-    carried = jnp.stack(tier_components)
-    prior_part = jnp.exp(-start_rate)[:, None, None] * prior_state
-    states = jnp.concatenate([carried, prior_part[None]], axis=0)
-    projected = jnp.einsum(
-        "tn,lhpn->tlhp", read_vec.astype(jnp.float32), states, precision=lax.Precision.HIGHEST
-    )
-    read_scale = read_weights[1:] * jnp.exp(-cum_rate)[None]
-    carried_out = jnp.einsum(
-        "lth,tlhp->thp", read_scale, projected, precision=lax.Precision.HIGHEST
-    )
+        carried_out = carried_out + read_weights[level][:, :, None] * projected
+    carried_out = carried_out * jnp.exp(-cum_rate)[:, :, None]
     mixed_out = (
         read_weights[0][:, :, None] * local_out
         + carried_out

time: 837 us -> 693 us (0.83)
  waiting for transfers between devices: 692 us -> 542 us
  other arithmetic: 20.6 us -> 8.63 us
  matrix products: 83.6 us -> 94.1 us
    all_gather x3 -> x4, waiting for transfers between devices: 492 us -> 304 us  [the longest x1 151 us: on_device(): lax.all_gather(w_value, 'ctx', axis=0, tiled=True, axis_index_groups=groups)]
    ppermute x0 -> x3, waiting for transfers between devices: none -> 132 us  [the longest x2 87.5 us: project(): back = lax.ppermute(other, 'ctx', across)]
    ppermute x6, waiting for transfers between devices: 198 us -> 80.8 us  [swapped(): lax.ppermute(value, axis, [(i, i ^ 1 << distance) for i in range(lax.axis...]
    all_to_all x0 -> x1, waiting for transfers between devices: none -> 24.3 us  [on_device(): token_part = lax.all_to_all(hidden_rows, 'tp', 0, 1, tiled=True)]
    dot_general x3 -> x8, matrix products: 63.6 us -> 75.7 us  [the longest x2 30.4 us: project(): mine = jnp.dot(rows[0], weight, preferred_element_type=jnp.float32)]
  transfers between devices with their start and end apart: 9 -> 14, of which waited for: 7 -> 9; matrix products, arithmetic and copies ran while one was open for 10% -> 15% of each run, Pallas kernels for 0% -> 0%
where the time goes in v1:
time: 693 us; the launch traced here: 690 us
  waiting for transfers between devices  542 us (78%)
  matrix products  94.1 us (14%)
  local copies, waits for them, and re-layouts  22.1 us (3%)
  between operations  13.5 us (2%)
  starting transfers between devices  9.69 us (1%)
  other arithmetic  8.63 us (1%)
    all_gather x1, waiting for transfers between devices, on_device(): lax.all_gather(w_value, 'ctx', axis=0, tiled=True, axis_index_groups=groups)  151 us
    all_gather x1, waiting for transfers between devices, on_device(): rows = lax.all_gather(jnp.stack([kept, taken]), 'tp', axis=1, tiled=True)  89.6 us
    ppermute x2, waiting for transfers between devices, project(): back = lax.ppermute(other, 'ctx', across)  87.5 us
    ppermute x6, waiting for transfers between devices, swapped(): lax.ppermute(value, axis, [(i, i ^ 1 << distance) for i in range(lax.axis...  80.8 us
    all_gather x1, waiting for transfers between devices, on_device(): lax.all_gather(w_gate, 'ctx', axis=0, tiled=True, axis_index_groups=groups)  63.2 us
    ppermute x1, waiting for transfers between devices, on_device(): taken = lax.ppermute(given, 'ctx', across)  44.3 us
    dot_general x2, matrix products, project(): mine = jnp.dot(rows[0], weight, preferred_element_type=jnp.float32)  30.4 us
    dot_general x2, matrix products, project(): jnp.dot(rows[1], weight, preferred_element_type=jnp.float32)  29.2 us
  transfers between devices with their start and end apart: 14, of which 9 were waited for; matrix products, arithmetic and copies ran while one was open for 15% of the time, Pallas kernels for 0%

profile of v1, /device:TPU:17, one launch (start us, length us, event | category | flops | bytes accessed | tf_op | source)
XLA Modules:
  0.0 689.9 jit_solution(7974122275637715766)
XLA Ops:
  6.5 3.7 all-to-all-start
  10.3 0.0 all-gather.5.cloned.1.call-start
  10.4 24.3 %all-to-all-done = bf16[4,128,2048]{2,1,0:T(8,128)(2,1)S(1)} async-done(((bf16[4,128,2048]{2,1,0:T(8,128)(2,1)}), bf16[4,128,2048]{2,1,0:T(8,128)(2,1)S(1)}, u32[]{:S(2)}, u32[]{:S(2)}) %all-to-all-start) | async-done | bytes 2097184 | tf_op jit(solution)/shard_map/all_to_all | solution.py:37
  34.6 1.3 copy-done.2
  36.0 3.0 copy.35
  39.0 0.1 dynamic-slice_bitcast_fusion
  39.1 0.1 collective-permute-start
  39.2 44.3 %collective-permute-done = bf16[128,4096]{0,1:T(8,128)(2,1)S(1)} collective-permute-done((bf16[128,4096]{0,1:T(8,128)(2,1)S(1)}, bf16[128,4096]{0,1:T(8,128)(2,1)S(1)}, u32[]{:S(2)}, u32[]{:S(2)}) %collective-permute-start) | collective-permute-done | bytes 1048608 | tf_op jit(solution)/shard_map/ppermute | solution.py:41
  83.5 1.5 pad_maximum_fusion
  85.0 0.0 all-gather.5.cloned.1.call-update
  85.0 0.0 all-gather.7.cloned.1.call-start
  85.1 0.7 all-gather.7.cloned.1.call-update
  85.8 0.0 all-gather.11.cloned.1.call-start
  85.8 0.7 all-gather.11.cloned.1.call-update
  86.5 0.0 all-gather.9.cloned.1.call-start
  86.6 89.6 %all-gather.5.cloned.1.call-done = bf16[2,512,4096]{1,2,0:T(8,128)(2,1)} async-done(((bf16[2,128,4096]{1,2,0:T(8,128)(2,1)}), bf16[2,512,4096]{1,2,0:T(8,128)(2,1)}) %all-gather.5.cloned.1.call-update) | async-done | bytes 8388624 | tf_op jit(solution)/shard_map/all_gather | solution.py:42
  176.1 150.8 %all-gather.7.cloned.1.call-done = bf16[4096,2048]{1,0:T(8,128)(2,1)} async-done(((bf16[1024,2048]{1,0:T(8,128)(2,1)}), bf16[4096,2048]{1,0:T(8,128)(2,1)}) %all-gather.7.cloned.1.call-update) | async-done | bytes 16777232 | tf_op jit(solution)/shard_map/all_gather | solution.py:36
  326.9 14.6 %fusion.12 = bf16[512,2048]{1,0:T(8,128)(2,1)} fusion(bf16[4096,2048]{1,0:T(8,128)(2,1)} %all-gather.7.cloned.1.call-done, bf16[2,512,4096]{1,2,0:T(8,128)(2,1)} %all-gather.5.cloned.1.call-done), kind=kOutput, calls=%fused_computation.24 | convolution fusion | flops 8590983168 | bytes 23068672 | tf_op jit(solution)/shard_map/dot_general | solution.py:46
  341.5 0.2 collective-permute-start.1
  341.7 1.2 reduce-window.6
  342.9 0.2 slice_reduce_fusion
  343.1 0.7 copy_bitcast_fusion.2
  343.8 0.2 slice_reduce_fusion.1
  344.0 2.4 fusion.50
  346.4 0.5 constant_dynamic-slice_fusion
  346.9 0.1 negate_exponential_fusion.1
  347.1 87.5 %collective-permute-done.1 = bf16[512,2048]{1,0:T(8,128)(2,1)} collective-permute-done((bf16[512,2048]{1,0:T(8,128)(2,1)}, bf16[512,2048]{1,0:T(8,128)(2,1)}, u32[]{:S(2)}, u32[]{:S(2)}) %collective-permute-start.1) | collective-permute-done | bytes 2097184 | tf_op jit(solution)/shard_map/ppermute | solution.py:47
  434.6 15.0 %add_convert_fusion.1 = bf16[512,2048]{1,0:T(8,128)(2,1)} fusion(bf16[512,2048]{1,0:T(8,128)(2,1)} %collective-permute-done.1, bf16[4096,2048]{1,0:T(8,128)(2,1)} %all-gather.7.cloned.1.call-done, bf16[2,512,4096]{1,2,0:T(8,128)(2,1)} %all-gather.5.cloned.1.call-done), kind=kOutput, calls=%fused_computation.16 | convolution fusion | flops 8593080320 | bytes 25165824 | tf_op jit(solution)/shard_map/dot_general | solution.py:48
  449.6 3.9 copy.36
  453.6 5.1 fusion.51
  458.7 63.2 %all-gather.11.cloned.1.call-done = bf16[4096,2048]{1,0:T(8,128)(2,1)} async-done(((bf16[1024,2048]{1,0:T(8,128)(2,1)}), bf16[4096,2048]{1,0:T(8,128)(2,1)}) %all-gather.11.cloned.1.call-update) | async-done | bytes 16777232 | tf_op jit(solution)/shard_map/all_gather | solution.py:43
  521.9 14.6 %fusion.13 = bf16[512,2048]{1,0:T(8,128)(2,1)} fusion(bf16[4096,2048]{1,0:T(8,128)(2,1)} %all-gather.11.cloned.1.call-done, bf16[2,512,4096]{1,2,0:T(8,128)(2,1)} %all-gather.5.cloned.1.call-done), kind=kOutput, calls=%fused_computation.25 | convolution fusion | flops 8590983168 | bytes 23068672 | tf_op jit(solution)/shard_map/dot_general | solution.py:46
  536.5 0.2 collective-permute-start.8
  536.7 0.5 constant_dynamic-slice_fusion.1
  537.4 0.1 mul.230
  537.4 0.5 collective-permute-done.3
  537.9 2.2 fusion.48
  540.1 0.1 collective-permute-start.4
  540.2 0.8 iota_compare_fusion
  541.0 0.7 slice_bitcast_fusion.20
  541.7 1.3 fusion.37
  543.0 1.4 collective-permute-start.5
  544.4 0.1 dynamic-slice.2
  544.5 61.0 %collective-permute-done.5 = f32[32]{0:T(128)S(1)} collective-permute-done((f32[32]{0:T(128)S(1)}, f32[32]{0:T(128)S(1)}, u32[]{:S(2)}, u32[]{:S(2)}) %collective-permute-start.5) | collective-permute-done | bytes 160 | tf_op jit(solution)/shard_map/ppermute | solution.py:13
  605.6 0.6 negate_exponential_fusion.2
  606.2 0.8 collective-permute-start.7
  607.0 0.1 dynamic-slice.3
  607.1 19.3 %collective-permute-done.7 = f32[32]{0:T(128)S(1)} collective-permute-done((f32[32]{0:T(128)S(1)}, f32[32]{0:T(128)S(1)}, u32[]{:S(2)}, u32[]{:S(2)}) %collective-permute-start.7) | collective-permute-done | bytes 160 | tf_op jit(solution)/shard_map/ppermute | solution.py:13
  626.4 0.5 fusion.41
  626.9 0.3 convert_element_type.87
  627.2 0.2 select_convert_fusion.4
  627.4 2.9 collective-permute-start.6
  630.2 15.3 %fusion.14 = f32[512,2048]{1,0:T(8,128)} fusion(bf16[512,2048]{1,0:T(8,128)(2,1)} %collective-permute-done.8, bf16[4096,2048]{1,0:T(8,128)(2,1)} %all-gather.11.cloned.1.call-done, bf16[2,512,4096]{1,2,0:T(8,128)(2,1)} %all-gather.5.cloned.1.call-done), kind=kOutput, calls=%fused_computation.26 | convolution fusion | flops 8594128896 | bytes 27262976 | tf_op jit(solution)/shard_map/dot_general | solution.py:48
  645.6 0.0 all-gather.9.cloned.1.call-update
  645.6 12.0 %fusion = f32[32,64,512]{2,1,0:T(8,128)} fusion(bf16[512,32,64]{0,2,1:T(8,128)(2,1)} %bitcast.101, f32[512,512]{1,0:T(8,128)S(1)} %copy-done.5, f32[32,512]{1,0:T(8,128)S(1)} %copy-done.7, pred[512,512]{1,0:T(8,128)(4,1)} %iota_compare_fusion), kind=kOutput, calls=%fused_computation.2 | convolution fusion | flops 1124073472 | bytes 7667712 | tf_op jit(solution)/shard_map/hts,shp->thp/dot_general | solution.py:66
  657.7 5.5 copy.41
  663.1 2.7 fusion.21
  665.8 2.8 fusion.18
  668.6 0.0 all-gather.9.cloned.1.call-done
  668.7 2.1 fusion.19
  670.9 0.9 copy-done.3
  671.8 8.6 %multiply_reduce_fusion = (f32[512,32]{0,1:T(8,128)S(1)}, f32[512,32,64]{0,2,1:T(8,128)S(1)}) fusion(f32[32]{0:T(128)S(1)} %copy-done.17, f32[512,32]{0,1:T(8,128)S(1)} %get-tuple-element.25, f32[512,32]{0,1:T(8,128)S(1)} %copy-done.11, f32[512,32,64]{0,2,1:T(8,128)S(1)} %fusion.19, f32[512,32]{0,1:T(8,128)S(1)} %copy-done.12, f32[512,32,64]{0,2,1:T(8,128)} %fusion.18, ...), kind=kOutput, calls=%fused_computation.14 | convolution fusion | flops 558874624 | bytes 30081280 | tf_op jit(solution)/shard_map/dot_general | solution.py:107
  680.5 0.5 multiply_convert_fusion.4
  681.0 2.4 copy.42
  (47 shorter events, 0.2 us)
Async XLA Ops:
  6.5 335.2 %copy-start = (f32[512,32]{0,1:T(8,128)S(1)}, f32[512,32]{0,1:T(8,128)}, u32[]{:S(2)}) copy-start(f32[512,32]{0,1:T(8,128)} %param.13) | copy-start | bytes 196612
  6.5 28.1 %all-to-all-start = ((bf16[4,128,2048]{2,1,0:T(8,128)(2,1)}), bf16[4,128,2048]{2,1,0:T(8,128)(2,1)S(1)}, u32[]{:S(2)}, u32[]{:S(2)}) async-start(bf16[4,128,2048]{2,1,0:T(8,128)(2,1)} %bitcast.99), calls=%async_computation | async-start | bytes 4194304 | tf_op jit(solution)/shard_map/all_to_all | solution.py:37
  10.3 165.9 %all-gather.5.cloned.1.call-start = ((), (), s32[]{:S(2)}) async-start(), calls=%async_computation.1 | async-start | bytes 10485760 | tf_op jit(solution)/shard_map/all_gather | solution.py:42
  34.6 1.3 copy-start.2
  39.1 44.4 %collective-permute-start = (bf16[128,4096]{0,1:T(8,128)(2,1)S(1)}, bf16[128,4096]{0,1:T(8,128)(2,1)S(1)}, u32[]{:S(2)}, u32[]{:S(2)}) collective-permute-start(bf16[128,4096]{0,1:T(8,128)(2,1)S(1)} %get-tuple-element.16), channel_id=1, source_target_pairs={{0,16},{4,20},{8,24},{12,28},{16,0},{20,4},{24,8},{28,12},{1,17},{... | collective-permute-start | bytes 3145736 | tf_op jit(solution)/shard_map/ppermute | solution.py:41
  85.0 241.9 %all-gather.7.cloned.1.call-start = ((), (), s32[]{:S(2)}) async-start(), calls=%async_computation.2 | async-start | bytes 20971520 | tf_op jit(solution)/shard_map/all_gather | solution.py:36
  85.8 436.1 %all-gather.11.cloned.1.call-start = ((), (), s32[]{:S(2)}) async-start(), calls=%async_computation.4 | async-start | bytes 20971520 | tf_op jit(solution)/shard_map/all_gather | solution.py:43
  86.5 582.1 %all-gather.9.cloned.1.call-start = ((), (), s32[]{:S(2)}) async-start(), calls=%async_computation.3 | async-start | bytes 1310720 | tf_op jit(solution)/shard_map/all_gather | solution.py:90
  341.5 93.1 %collective-permute-start.1 = (bf16[512,2048]{1,0:T(8,128)(2,1)}, bf16[512,2048]{1,0:T(8,128)(2,1)}, u32[]{:S(2)}, u32[]{:S(2)}) collective-permute-start(bf16[512,2048]{1,0:T(8,128)(2,1)} %fusion.12), channel_id=1, source_target_pairs={{0,16},{4,20},{8,24},{12,28},{16,0},{20,4},{24,8},{28,12},{1,17},{... | collective-permute-start | bytes 6291464 | tf_op jit(solution)/shard_map/ppermute | solution.py:47
  458.7 78.7 %copy-start.15 = (f32[2048]{0:T(1024)S(1)}, f32[2048]{0:T(1024)}, u32[]{:S(2)}) copy-start(f32[2048]{0:T(1024)} %param.17) | copy-start | bytes 24580
  458.7 79.2 %collective-permute-start.2 = (bf16[32,64,256]{2,1,0:T(8,128)(2,1)}, bf16[32,64,256]{2,1,0:T(8,128)(2,1)S(1)}, u32[]{:S(2)}, u32[]{:S(2)}) collective-permute-start(bf16[32,64,256]{2,1,0:T(8,128)(2,1)} %get-tuple-element.31), channel_id=1, source_target_pairs={{0,4},{4,0},{8,12},{12,8},{16,20},{20,16},{24,28},{28,24},{1,5},{5... | collective-permute-start | bytes 3145736 | tf_op jit(solution)/shard_map/ppermute | solution.py:13
  536.5 93.7 %collective-permute-start.8 = (bf16[512,2048]{1,0:T(8,128)(2,1)}, bf16[512,2048]{1,0:T(8,128)(2,1)}, u32[]{:S(2)}, u32[]{:S(2)}) collective-permute-start(bf16[512,2048]{1,0:T(8,128)(2,1)} %fusion.13), channel_id=1, source_target_pairs={{0,16},{4,20},{8,24},{12,28},{16,0},{20,4},{24,8},{28,12},{1,17},{... | collective-permute-start | bytes 6291464 | tf_op jit(solution)/shard_map/ppermute | solution.py:47
  536.7 1.2 collective-permute-start.3
  536.7 4.3 copy-start.6
  540.1 86.8 %collective-permute-start.4 = (bf16[32,64,256]{2,1,0:T(8,128)(2,1)S(1)}, bf16[32,64,256]{2,1,0:T(8,128)(2,1)S(1)}, u32[]{:S(2)}, u32[]{:S(2)}) collective-permute-start(bf16[32,64,256]{2,1,0:T(8,128)(2,1)S(1)} %get-tuple-element.11), channel_id=1, source_target_pairs={{0,8},{4,12},{8,0},{12,4},{16,24},{20,28},{24,16},{28,20},{1,9},{5... | collective-permute-start | bytes 3145736 | tf_op jit(solution)/shard_map/ppermute | solution.py:13
  543.0 62.5 %collective-permute-start.5 = (f32[32]{0:T(128)S(1)}, f32[32]{0:T(128)S(1)}, u32[]{:S(2)}, u32[]{:S(2)}) collective-permute-start(f32[32]{0:T(128)S(1)} %get-tuple-element.10), channel_id=1, source_target_pairs={{0,8},{4,12},{8,0},{12,4},{16,24},{20,28},{24,16},{28,20},{1,9},{5... | collective-permute-start | bytes 392 | tf_op jit(solution)/shard_map/ppermute | solution.py:13
  606.2 20.2 %collective-permute-start.7 = (f32[32]{0:T(128)S(1)}, f32[32]{0:T(128)S(1)}, u32[]{:S(2)}, u32[]{:S(2)}) collective-permute-start(f32[32]{0:T(128)S(1)} %get-tuple-element.28), channel_id=1, source_target_pairs={{0,16},{4,20},{8,24},{12,28},{16,0},{20,4},{24,8},{28,12},{1,17},{... | collective-permute-start | bytes 392 | tf_op jit(solution)/shard_map/ppermute | solution.py:13
  627.3 18.3 %copy-start.5 = (f32[512,512]{1,0:T(8,128)S(1)}, f32[512,512]{1,0:T(8,128)}, u32[]{:S(2)}) copy-start(f32[512,512]{1,0:T(8,128)} %fusion.37) | copy-start | bytes 3145732
  627.3 18.3 %copy-start.7 = (f32[32,512]{1,0:T(8,128)S(1)}, f32[32,512]{1,0:T(8,128)}, u32[]{:S(2)}) copy-start(f32[32,512]{1,0:T(8,128)} %get-tuple-element.22) | copy-start | bytes 196612
  627.4 18.2 %collective-permute-start.6 = (bf16[8,64,256]{2,1,0:T(8,128)(2,1)S(1)}, bf16[8,64,256]{2,1,0:T(8,128)(2,1)}, u32[]{:S(2)}, u32[]{:S(2)}) collective-permute-start(bf16[8,64,256]{2,1,0:T(8,128)(2,1)S(1)} %select_convert_fusion.4), channel_id=1, source_target_pairs={{0,16},{4,20},{8,24},{12,28},{16,0},{20,4},{24,8},{28,12},{1,17},{... | collective-permute-start | bytes 786440 | tf_op jit(solution)/shard_map/ppermute | solution.py:13
  663.1 2.7 copy-start.14
  665.8 2.8 copy-start.13
  665.8 5.0 copy-start.11
  665.8 5.0 copy-start.12
  668.6 2.2 copy-start.4
  668.6 2.2 copy-start.8
  668.6 2.2 copy-start.9
  668.6 2.3 copy-start.10
  668.6 2.3 copy-start.16
  668.6 2.3 copy-start.17
  668.6 3.2 copy-start.3
  680.4 2.9 copy-start.1
Sparse Core Ops, SparseCore 0:
  85.1 90.9 all-gather.4
  177.7 149.1 all-gather.6
  328.5 193.4 all-gather.10
  645.7 19.8 all-gather.8

commit v2 on v1

--- a/solution.py
+++ b/solution.py
@@ -1,16 +1,69 @@
+import functools
+
 import jax
 import jax.numpy as jnp
 from jax import lax
+from jax.experimental import pallas as pl
+from jax.experimental.pallas import tpu as pltpu
+
 from jax.sharding import PartitionSpec as P
 
 HEAD_DIM = 64
-STATE = 256
 HPG = 32
 LEVELS = 6
 
 
 def swapped(value, axis, distance):
     return lax.ppermute(value, axis, [(i, i ^ 1 << distance) for i in range(lax.axis_size(axis))])
+
+
+def project_kernel(count, added, place_ref, *refs):
+    rows, weights = refs[:count], refs[count : 2 * count]
+    total = jnp.dot(rows[0][...], weights[0][...], preferred_element_type=jnp.float32)
+    for row, weight in zip(rows[1:], weights[1:]):
+        total = total + jnp.dot(row[...], weight[...], preferred_element_type=jnp.float32)
+    if added:
+        total = total + refs[2 * count][...].astype(jnp.float32)
+    refs[-1][...] = total.astype(jnp.bfloat16)
+
+
+def project(place, rows, blocks, extra=None):
+    tok_rows = rows.shape[0]
+    depth, width = blocks[0].shape
+    tile = min(width, 256)
+    masks = range(len(blocks))
+    in_specs = [
+        pl.BlockSpec((tok_rows, depth), functools.partial(lambda m, i, p: (0, p[0] ^ m), m))
+        for m in masks
+    ]
+    in_specs += [pl.BlockSpec((depth, tile), lambda i, p: (0, i)) for _ in masks]
+    operands = [rows] * len(blocks) + list(blocks)
+    if extra is not None:
+        in_specs.append(pl.BlockSpec((tok_rows, tile), lambda i, p: (0, i)))
+        operands.append(extra)
+    flops = 2 * tok_rows * depth * len(blocks) * width
+    moved = 2 * (rows.size + len(blocks) * depth * width + tok_rows * width)
+    return pl.pallas_call(
+        functools.partial(project_kernel, len(blocks), extra is not None),
+        out_shape=jax.ShapeDtypeStruct((tok_rows, width), jnp.bfloat16),
+        grid_spec=pltpu.PrefetchScalarGridSpec(
+            num_scalar_prefetch=1,
+            grid=(width // tile,),
+            in_specs=in_specs,
+            out_specs=pl.BlockSpec((tok_rows, tile), lambda i, p: (0, i)),
+        ),
+        compiler_params=pltpu.CompilerParams(vmem_limit_bytes=40 * 1024 * 1024),
+        cost_estimate=pl.CostEstimate(flops=flops, bytes_accessed=moved, transcendentals=0),
+    )(place, *operands)
+
+
+def gather_blocks(weight, half):
+    blocks = {0: weight}
+    bits = half.bit_length() - 1
+    for bit_pos in [*range(1, bits), 0][-bits:] if bits else []:
+        for mask in list(blocks):
+            blocks[mask | 1 << bit_pos] = swapped(blocks[mask], "ctx", bit_pos)
+    return [blocks[mask] for mask in range(half)]
 
 
 def on_device(
@@ -33,23 +86,25 @@
     upper_half = my_block // half
     groups = [list(range(half)), list(range(half, ctx_size))]
     across = [(i, (i + half) % ctx_size) for i in range(ctx_size)]
-    w_value_half = lax.all_gather(w_value, "ctx", axis=0, tiled=True, axis_index_groups=groups)
+    value_blocks = gather_blocks(w_value, half)
     token_part = lax.all_to_all(hidden_rows, "tp", 0, 1, tiled=True)
     depth = token_part.shape[1] // 2
     kept = lax.dynamic_slice_in_dim(token_part, upper_half * depth, depth, 1)
     given = lax.dynamic_slice_in_dim(token_part, (1 - upper_half) * depth, depth, 1)
     taken = lax.ppermute(given, "ctx", across)
-    rows = lax.all_gather(jnp.stack([kept, taken]), "tp", axis=1, tiled=True)
-    w_gate_half = lax.all_gather(w_gate, "ctx", axis=0, tiled=True, axis_index_groups=groups)
-
-    def project(weight):
-        other = jnp.dot(rows[1], weight, preferred_element_type=jnp.float32).astype(jnp.bfloat16)
-        back = lax.ppermute(other, "ctx", across)
-        mine = jnp.dot(rows[0], weight, preferred_element_type=jnp.float32)
-        return (mine + back.astype(jnp.float32)).astype(jnp.bfloat16)
-
-    values_proj = project(w_value_half)
-    gates_proj = project(w_gate_half)
+    rows_mine = lax.all_gather(kept, "tp", axis=0, tiled=True)
+    rows_other = lax.all_gather(taken, "tp", axis=0, tiled=True)
+    gate_start, far_block = lax.optimization_barrier((w_gate, value_blocks[half // 2]))
+    value_blocks[half // 2] = far_block
+    gate_blocks = gather_blocks(gate_start, half)
+    place = jnp.reshape(my_block % half, (1,)).astype(jnp.int32)
+    value_back = lax.ppermute(project(place, rows_other, value_blocks), "ctx", across)
+    gate_other, value_back = lax.optimization_barrier(
+        (project(place, rows_other, gate_blocks), value_back)
+    )
+    gate_back = lax.ppermute(gate_other, "ctx", across)
+    values_proj = project(place, rows_mine, value_blocks, value_back)
+    gates_proj = project(place, rows_mine, gate_blocks, gate_back)
     values3 = values_proj.reshape(tok_rows, head_count, HEAD_DIM)
     group_index = lax.axis_index("tp") * head_count // HPG
     write_vec = lax.dynamic_index_in_dim(state_proj[:, 0], group_index, 1, keepdims=False)
@@ -134,6 +189,7 @@
         P("tp"),
     )
     out_specs = P("ctx", "tp")
+
     return jax.shard_map(
         on_device, mesh=mesh, in_specs=in_specs, out_specs=out_specs, check_vma=False
     )

time: 693 us -> 550 us (0.79)
  waiting for transfers between devices: 542 us -> 378 us
  matrix products: 94.1 us -> 36 us
  Pallas kernels: 0 us -> 51.8 us
  starting transfers between devices: 9.69 us -> 21.9 us
  local copies, waits for them, and re-layouts: 22.1 us -> 31.3 us
    all_gather x3 -> x2, waiting for transfers between devices: 304 us -> 0.02 us  [the longest x1 0.02 us: on_device(): rows_other = lax.all_gather(taken, 'tp', axis=0, tiled=True)]
    ppermute x6 -> x12, waiting for transfers between devices: 80.8 us -> 241 us  [swapped(): lax.ppermute(value, axis, [(i, i ^ 1 << distance) for i in range(lax.axis...]
    dot_general x4 -> x0, matrix products: 59.5 us -> none  [the longest x2 30.4 us: project(): mine = jnp.dot(rows[0], weight, preferred_element_type=jnp.float32)]
    pallas_call x0 -> x4, Pallas kernels: none -> 51.8 us  [project(): pl.pallas_call(functools.partial(project_kernel, len(blocks), extra is no...]
    ppermute x2, waiting for transfers between devices: 87.5 us -> 68.9 us  [the longest x1 68.9 us: on_device(): lax.ppermute(project(place, rows_other, value_blocks), 'ctx', across)]
    unnamed x37 -> x47, local copies, waits for them, and re-layouts: 2.37 us -> 14.5 us
    ppermute x6 -> x12, starting transfers between devices: 5.24 us -> 16.9 us  [swapped(): lax.ppermute(value, axis, [(i, i ^ 1 << distance) for i in range(lax.axis...]
  transfers between devices with their start and end apart: 14 -> 19, of which waited for: 9 -> 8; matrix products, arithmetic and copies ran while one was open for 15% -> 6% of each run, Pallas kernels for 0% -> 7%
where the time goes in v2:
time: 550 us; the launch traced here: 543 us
  waiting for transfers between devices  378 us (69%)
  Pallas kernels  51.8 us (9%)
  matrix products  36 us (7%)
  local copies, waits for them, and re-layouts  31.3 us (6%)
  starting transfers between devices  21.9 us (4%)
  between operations  13.5 us (2%)
  other arithmetic  11.2 us (2%)
    ppermute x12, waiting for transfers between devices, swapped(): lax.ppermute(value, axis, [(i, i ^ 1 << distance) for i in range(lax.axis...  241 us
    ppermute x1, waiting for transfers between devices, on_device(): lax.ppermute(project(place, rows_other, value_blocks), 'ctx', across)  68.9 us
    pallas_call x4, Pallas kernels, project(): pl.pallas_call(functools.partial(project_kernel, len(blocks), extra is no...  51.8 us
    ppermute x1, waiting for transfers between devices, on_device(): taken = lax.ppermute(given, 'ctx', across)  43 us
    all_to_all x1, waiting for transfers between devices, on_device(): token_part = lax.all_to_all(hidden_rows, 'tp', 0, 1, tiled=True)  24.3 us
    ppermute x12, starting transfers between devices, swapped(): lax.ppermute(value, axis, [(i, i ^ 1 << distance) for i in range(lax.axis...  16.9 us
    dot_general x1, matrix products, on_device(): jnp.einsum('hts,shp->thp', mixing, values3, preferred_element_type=jnp.fl...  15 us
    unnamed x47, local copies, waits for them, and re-layouts  14.5 us
  transfers between devices with their start and end apart: 19, of which 8 were waited for; matrix products, arithmetic and copies ran while one was open for 6% of the time, Pallas kernels for 7%

profile of v2, /device:TPU:17, one launch (start us, length us, event | category | flops | bytes accessed | tf_op | source)
XLA Modules:
  0.0 543.3 jit_solution(5001161169769724329)
XLA Ops:
  6.5 3.7 all-to-all-start
  10.4 24.3 %all-to-all-done = bf16[4,128,2048]{2,1,0:T(8,128)(2,1)S(1)} async-done(((bf16[4,128,2048]{2,1,0:T(8,128)(2,1)}), bf16[4,128,2048]{2,1,0:T(8,128)(2,1)S(1)}, u32[]{:S(2)}, u32[]{:S(2)}) %all-to-all-start) | async-done | bytes 2097184 | tf_op jit(solution)/shard_map/all_to_all | solution.py:90
  34.6 0.1 copy.52
  34.8 1.1 constant_dynamic-slice_fusion.2
  35.9 1.3 collective-permute-start.1
  37.2 43.0 %collective-permute-done.3 = bf16[128,4096]{1,0:T(8,128)(2,1)S(1)} collective-permute-done((bf16[128,4096]{1,0:T(8,128)(2,1)S(1)}, bf16[128,4096]{1,0:T(8,128)(2,1)S(1)}, u32[]{:S(2)}, u32[]{:S(2)}) %collective-permute-start.3) | collective-permute-done | bytes 1048608 | tf_op jit(solution)/shard_map/ppermute | solution.py:94
  80.2 1.0 copy-done.17
  81.3 67.9 %collective-permute-done.1.refs_6_ = bf16[1024,2048]{1,0:T(8,128)(2,1)} collective-permute-done((bf16[1024,2048]{1,0:T(8,128)(2,1)}, bf16[1024,2048]{1,0:T(8,128)(2,1)}, u32[]{:S(2)}, u32[]{:S(2)}) %collective-permute-start.1) | collective-permute-done | bytes 4194336 | tf_op jit(solution)/shard_map/ppermute | solution.py:17
  149.1 1.4 collective-permute-start.5
  150.5 2.8 collective-permute-start
  153.4 0.6 collective-permute-start.4
  154.0 85.4 %collective-permute-done.5.refs_6_ = bf16[1024,2048]{1,0:T(8,128)(2,1)} collective-permute-done((bf16[1024,2048]{1,0:T(8,128)(2,1)}, bf16[1024,2048]{1,0:T(8,128)(2,1)}, u32[]{:S(2)}, u32[]{:S(2)}) %collective-permute-start.5) | collective-permute-done | bytes 4194336 | tf_op jit(solution)/shard_map/ppermute | solution.py:17
  239.3 3.1 collective-permute-start.6
  242.5 1.2 reduce-window.6
  243.7 2.2 copy-done.4
  245.9 13.7 %shard_map.92 = bf16[512,2048]{1,0:T(8,128)(2,1)} custom-call(s32[1]{0:T(128)} %bitcast.1.place_ref, bf16[512,4096]{1,0:T(8,128)(2,1)S(1)} %copy-done.4, bf16[512,4096]{1,0:T(8,128)(2,1)S(1)} %copy-done.4, bf16[512,4096]{1,0:T(8,128)(2,1)S(1)} %copy-done.4, bf16[512,4096]{1,0:T(8,128)(2,1)S(1)} %copy-done.4, bf16[1024,2048]{1,0:T(8,128)(2,1)} %refs_4_.4, ...), custom_call_target="tpu_custom_call" | custom-call | flops 8589934592 | bytes 23068672 | tf_op jit(solution)/shard_map/pallas_call | solution.py:46
  259.6 1.1 collective-permute-start.7
  260.8 0.2 slice_reduce_fusion
  261.0 0.1 copy_bitcast_fusion.2
  261.1 0.2 slice_reduce_fusion.1
  261.2 3.4 fusion.42
  264.7 0.5 constant_dynamic-slice_fusion
  265.2 0.8 negate_exponential_fusion
  266.2 2.2 copy-done.6
  268.3 12.4 %shard_map.91 = bf16[512,2048]{1,0:T(8,128)(2,1)S(1)} custom-call(s32[1]{0:T(128)} %bitcast.1.place_ref, bf16[512,4096]{1,0:T(8,128)(2,1)S(1)} %copy-done.5, bf16[512,4096]{1,0:T(8,128)(2,1)S(1)} %copy-done.5, bf16[512,4096]{1,0:T(8,128)(2,1)S(1)} %copy-done.5, bf16[512,4096]{1,0:T(8,128)(2,1)S(1)} %copy-done.5, bf16[1024,2048]{1,0:T(8,128)(2,1)S(1)} %copy-done.6, ...), custom_call_target="tpu_custom_call" | custom-call | flops 8589934592 | bytes 23068672 | tf_op jit(solution)/shard_map/pallas_call | solution.py:46
  280.8 1.3 copy-done.8
  282.1 68.9 %collective-permute-done.7.refs_8_ = bf16[512,2048]{1,0:T(8,128)(2,1)S(1)} collective-permute-done((bf16[512,2048]{1,0:T(8,128)(2,1)}, bf16[512,2048]{1,0:T(8,128)(2,1)S(1)}, u32[]{:S(2)}, u32[]{:S(2)}) %collective-permute-start.7) | collective-permute-done | bytes 2097184 | tf_op jit(solution)/shard_map/ppermute | solution.py:101
  351.0 1.3 copy-done.10
  352.3 2.2 copy-done.2
  354.5 1.6 copy-done.11
  356.1 12.8 %shard_map.93 = bf16[512,2048]{1,0:T(8,128)(2,1)S(1)} custom-call(s32[1]{0:T(128)} %bitcast.1.place_ref, bf16[512,4096]{1,0:T(8,128)(2,1)S(1)} %copy-done.2, bf16[512,4096]{1,0:T(8,128)(2,1)S(1)} %copy-done.2, bf16[512,4096]{1,0:T(8,128)(2,1)S(1)} %copy-done.2, bf16[512,4096]{1,0:T(8,128)(2,1)S(1)} %copy-done.2, bf16[1024,2048]{1,0:T(8,128)(2,1)} %refs_4_.4, ...), custom_call_target="tpu_custom_call" | custom-call | flops 8589934592 | bytes 23068672 | tf_op jit(solution)/shard_map/pallas_call | solution.py:46
  368.9 2.6 copy.39
  371.5 5.2 fusion.43
  376.6 0.9 collective-permute-start.8
  377.5 0.1 collective-permute-start.9
  377.6 2.4 collective-permute-done.9
  380.0 3.8 fusion.40
  383.8 3.0 collective-permute-start.10
  386.9 1.3 constant_dynamic-slice_fusion.1
  388.2 1.1 copy.47
  389.3 1.7 slice_bitcast_fusion.4
  391.0 2.3 fusion.30
  393.4 1.4 collective-permute-start.11
  394.8 0.1 dynamic-slice.2
  394.8 60.5 %collective-permute-done.11 = f32[32]{0:T(128)S(1)} collective-permute-done((f32[32]{0:T(128)S(1)}, f32[32]{0:T(128)S(1)}, u32[]{:S(2)}, u32[]{:S(2)}) %collective-permute-start.11) | collective-permute-done | bytes 160 | tf_op jit(solution)/shard_map/ppermute | solution.py:17
  455.3 0.5 negate_exponential_fusion.2
  455.9 0.1 dynamic-slice.3
  455.9 1.5 convert_element_type.66
  457.4 1.9 select_convert_fusion.4
  459.3 0.8 iota_compare_fusion
  460.1 2.4 collective-permute-start.13
  462.5 0.1 mul.230
  462.6 25.2 %collective-permute-done.13 = f32[32]{0:T(128)S(1)} collective-permute-done((f32[32]{0:T(128)S(1)}, f32[32]{0:T(128)S(1)}, u32[]{:S(2)}, u32[]{:S(2)}) %collective-permute-start.13) | collective-permute-done | bytes 160 | tf_op jit(solution)/shard_map/ppermute | solution.py:17
  487.9 4.5 fusion.13
  492.4 2.8 fusion.14
  495.1 0.7 copy-done.3
  495.8 12.8 %shard_map.94 = bf16[512,2048]{1,0:T(8,128)(2,1)S(1)} custom-call(s32[1]{0:T(128)} %bitcast.1.place_ref, bf16[512,4096]{1,0:T(8,128)(2,1)S(1)} %copy-done.3, bf16[512,4096]{1,0:T(8,128)(2,1)S(1)} %copy-done.3, bf16[512,4096]{1,0:T(8,128)(2,1)S(1)} %copy-done.3, bf16[512,4096]{1,0:T(8,128)(2,1)S(1)} %copy-done.3, bf16[1024,2048]{1,0:T(8,128)(2,1)S(1)} %copy-done.7, ...), custom_call_target="tpu_custom_call" | custom-call | flops 8589934592 | bytes 23068672 | tf_op jit(solution)/shard_map/pallas_call | solution.py:46
  508.6 3.0 copy.44
  511.6 4.1 fusion.11
  515.8 2.1 fusion.12
  517.9 1.0 copy-done.12
  518.9 15.0 %multiply_reduce_fusion = (f32[512,32]{0,1:T(8,128)S(1)}, f32[512,32,64]{0,2,1:T(8,128)S(1)}) fusion(f32[512,32,64]{0,2,1:T(8,128)} %bitcast.71, bf16[512,32,64]{0,2,1:T(8,128)(2,1)S(1)} %bitcast.74, f32[32]{0:T(128)S(1)} %copy-done.22, f32[512,32]{0,1:T(8,128)S(1)} %copy-done.18, f32[512,32,64]{0,2,1:T(8,128)S(1)} %copy-done.12, ...), kind=kOutput, calls=%fused_computation.12 | convolution fusion | flops 1145028608 | bytes 29098112 | tf_op jit(solution)/shard_map/hts,shp->thp/dot_general | solution.py:121
  533.9 0.5 multiply_convert_fusion.4
  534.4 2.4 copy.45
  (65 shorter events, 0.4 us)
Async XLA Ops:
  6.5 235.9 %copy-start = (f32[512,32]{0,1:T(8,128)S(1)}, f32[512,32]{0,1:T(8,128)}, u32[]{:S(2)}) copy-start(f32[512,32]{0,1:T(8,128)} %param.13) | copy-start | bytes 196612
  6.5 28.1 %all-to-all-start = ((bf16[4,128,2048]{2,1,0:T(8,128)(2,1)}), bf16[4,128,2048]{2,1,0:T(8,128)(2,1)S(1)}, u32[]{:S(2)}, u32[]{:S(2)}) async-start(bf16[4,128,2048]{2,1,0:T(8,128)(2,1)} %bitcast.72), calls=%async_computation | async-start | bytes 4194304 | tf_op jit(solution)/shard_map/all_to_all | solution.py:90
  10.3 233.4 %all-gather.6.cloned.1.call-start = ((), (), s32[]{:S(2)}) async-start(), calls=%async_computation.2 | async-start | bytes 5242880 | tf_op jit(solution)/shard_map/all_gather | solution.py:96
  35.9 44.3 %collective-permute-start.3 = (bf16[128,4096]{1,0:T(8,128)(2,1)S(1)}, bf16[128,4096]{1,0:T(8,128)(2,1)S(1)}, u32[]{:S(2)}, u32[]{:S(2)}) collective-permute-start(bf16[128,4096]{1,0:T(8,128)(2,1)S(1)} %get-tuple-element.21), channel_id=1, source_target_pairs={{0,16},{4,20},{8,24},{12,28},{16,0},{20,4},{24,8},{28,12},{1,17},{... | collective-permute-start | bytes 3145736 | tf_op jit(solution)/shard_map/ppermute | solution.py:94
  35.9 113.2 %collective-permute-start.1 = (bf16[1024,2048]{1,0:T(8,128)(2,1)}, bf16[1024,2048]{1,0:T(8,128)(2,1)}, u32[]{:S(2)}, u32[]{:S(2)}) collective-permute-start(bf16[1024,2048]{1,0:T(8,128)(2,1)} %refs_4_.4), channel_id=1, source_target_pairs={{0,8},{4,12},{8,0},{12,4},{16,24},{20,28},{24,16},{28,20},{1,9},{5... | collective-permute-start | bytes 12582920 | tf_op jit(solution)/shard_map/ppermute | solution.py:17
  80.2 1.0 copy-start.17
  81.2 271.1 %all-gather.4.cloned.1.call-start = ((), (), s32[]{:S(2)}) async-start(), calls=%async_computation.1 | async-start | bytes 5242880 | tf_op jit(solution)/shard_map/all_gather | solution.py:95
  149.1 90.2 %collective-permute-start.5 = (bf16[1024,2048]{1,0:T(8,128)(2,1)}, bf16[1024,2048]{1,0:T(8,128)(2,1)}, u32[]{:S(2)}, u32[]{:S(2)}) collective-permute-start(bf16[1024,2048]{1,0:T(8,128)(2,1)} %refs_4_.5), channel_id=1, source_target_pairs={{0,8},{4,12},{8,0},{12,4},{16,24},{20,28},{24,16},{28,20},{1,9},{5... | collective-permute-start | bytes 12582920 | tf_op jit(solution)/shard_map/ppermute | solution.py:17
  150.5 93.1 %collective-permute-start = (bf16[1024,2048]{1,0:T(8,128)(2,1)}, bf16[1024,2048]{1,0:T(8,128)(2,1)}, u32[]{:S(2)}, u32[]{:S(2)}) collective-permute-start(bf16[1024,2048]{1,0:T(8,128)(2,1)} %refs_4_.4), channel_id=1, source_target_pairs={{0,4},{4,0},{8,12},{12,8},{16,20},{20,16},{24,28},{28,24},{1,5},{5... | collective-permute-start | bytes 12582920 | tf_op jit(solution)/shard_map/ppermute | solution.py:17
  153.3 90.3 %collective-permute-start.2 = (bf16[1024,2048]{1,0:T(8,128)(2,1)}, bf16[1024,2048]{1,0:T(8,128)(2,1)}, u32[]{:S(2)}, u32[]{:S(2)}) collective-permute-start(bf16[1024,2048]{1,0:T(8,128)(2,1)} %collective-permute-done.1.refs_6_), channel_id=1, source_target_pairs={{0,4},{4,0},{8,12},{12,8},{16,20},{20,16},{24,28},{28,24},{1,5},{5... | collective-permute-start | bytes 12582920 | tf_op jit(solution)/shard_map/ppermute | solution.py:17
  153.3 362.4 %all-gather.8.cloned.1.call-start = ((), (), s32[]{:S(2)}) async-start(), calls=%async_computation.3 | async-start | bytes 1310720 | tf_op jit(solution)/shard_map/all_gather | solution.py:145
  153.4 112.7 %collective-permute-start.4 = (bf16[1024,2048]{1,0:T(8,128)(2,1)}, bf16[1024,2048]{1,0:T(8,128)(2,1)}, u32[]{:S(2)}, u32[]{:S(2)}) collective-permute-start(bf16[1024,2048]{1,0:T(8,128)(2,1)} %refs_4_.5), channel_id=1, source_target_pairs={{0,4},{4,0},{8,12},{12,8},{16,20},{20,16},{24,28},{28,24},{1,5},{5... | collective-permute-start | bytes 12582920 | tf_op jit(solution)/shard_map/ppermute | solution.py:17
  239.3 26.8 %collective-permute-start.6 = (bf16[1024,2048]{1,0:T(8,128)(2,1)}, bf16[1024,2048]{1,0:T(8,128)(2,1)}, u32[]{:S(2)}, u32[]{:S(2)}) collective-permute-start(bf16[1024,2048]{1,0:T(8,128)(2,1)} %collective-permute-done.5.refs_6_), channel_id=1, source_target_pairs={{0,4},{4,0},{8,12},{12,8},{16,20},{20,16},{24,28},{28,24},{1,5},{5... | collective-permute-start | bytes 12582920 | tf_op jit(solution)/shard_map/ppermute | solution.py:17
  243.7 2.2 copy-start.4
  259.6 91.4 %collective-permute-start.7 = (bf16[512,2048]{1,0:T(8,128)(2,1)}, bf16[512,2048]{1,0:T(8,128)(2,1)S(1)}, u32[]{:S(2)}, u32[]{:S(2)}) collective-permute-start(bf16[512,2048]{1,0:T(8,128)(2,1)} %shard_map.92), channel_id=1, source_target_pairs={{0,16},{4,20},{8,24},{12,28},{16,0},{20,4},{24,8},{28,12},{1,17},{... | collective-permute-start | bytes 6291464 | tf_op jit(solution)/shard_map/ppermute | solution.py:101
  261.0 5.2 copy-start.5
  265.2 0.9 copy-start.13
  266.1 2.2 copy-start.6
  280.7 1.3 copy-start.8
  351.0 1.3 copy-start.10
  352.3 2.2 copy-start.2
  354.5 1.6 copy-start.11
  376.6 10.2 %copy-start.9 = (bf16[512,2048]{1,0:T(8,128)(2,1)S(1)}, bf16[512,2048]{1,0:T(8,128)(2,1)}, u32[]{:S(2)}) copy-start(bf16[512,2048]{1,0:T(8,128)(2,1)} %copy-done.8) | copy-start | bytes 6291460
  376.6 3.4 collective-permute-start.8
  377.5 2.5 collective-permute-start.9
  377.6 9.3 %copy-start.14 = (bf16[512,1,4,256]{3,2,1,0:T(4,128)(2,1)S(1)}, bf16[512,1,4,256]{3,2,1,0:T(4,128)(2,1)}, u32[]{:S(2)}) copy-start(bf16[512,1,4,256]{3,2,1,0:T(4,128)(2,1)} %get-tuple-element.20) | copy-start | bytes 3145732
  383.8 72.1 %collective-permute-start.10 = (bf16[32,64,256]{2,1,0:T(8,128)(2,1)}, bf16[32,64,256]{2,1,0:T(8,128)(2,1)}, u32[]{:S(2)}, u32[]{:S(2)}) collective-permute-start(bf16[32,64,256]{2,1,0:T(8,128)(2,1)} %get-tuple-element.17), channel_id=1, source_target_pairs={{0,8},{4,12},{8,0},{12,4},{16,24},{20,28},{24,16},{28,20},{1,9},{5... | collective-permute-start | bytes 3145736 | tf_op jit(solution)/shard_map/ppermute | solution.py:17
  386.9 108.3 %collective-permute-start.14 = (bf16[512,2048]{1,0:T(8,128)(2,1)S(1)}, bf16[512,2048]{1,0:T(8,128)(2,1)}, u32[]{:S(2)}, u32[]{:S(2)}) collective-permute-start(bf16[512,2048]{1,0:T(8,128)(2,1)S(1)} %copy-done.9), channel_id=1, source_target_pairs={{0,16},{4,20},{8,24},{12,28},{16,0},{20,4},{24,8},{28,12},{1,17},{... | collective-permute-start | bytes 6291464 | tf_op jit(solution)/shard_map/ppermute | solution.py:105
  386.9 75.6 %copy-start.21 = (f32[2048]{0:T(1024)S(1)}, f32[2048]{0:T(1024)}, u32[]{:S(2)}) copy-start(f32[2048]{0:T(1024)} %param.17) | copy-start | bytes 24580
  393.4 62.0 %collective-permute-start.11 = (f32[32]{0:T(128)S(1)}, f32[32]{0:T(128)S(1)}, u32[]{:S(2)}, u32[]{:S(2)}) collective-permute-start(f32[32]{0:T(128)S(1)} %get-tuple-element.16), channel_id=1, source_target_pairs={{0,8},{4,12},{8,0},{12,4},{16,24},{20,28},{24,16},{28,20},{1,9},{5... | collective-permute-start | bytes 392 | tf_op jit(solution)/shard_map/ppermute | solution.py:17
  459.3 28.5 %collective-permute-start.12 = (bf16[8,64,256]{2,1,0:T(8,128)(2,1)}, bf16[8,64,256]{2,1,0:T(8,128)(2,1)}, u32[]{:S(2)}, u32[]{:S(2)}) collective-permute-start(bf16[8,64,256]{2,1,0:T(8,128)(2,1)} %select_convert_fusion.4), channel_id=1, source_target_pairs={{0,16},{4,20},{8,24},{12,28},{16,0},{20,4},{24,8},{28,12},{1,17},{... | collective-permute-start | bytes 786440 | tf_op jit(solution)/shard_map/ppermute | solution.py:17
  460.1 27.7 %collective-permute-start.13 = (f32[32]{0:T(128)S(1)}, f32[32]{0:T(128)S(1)}, u32[]{:S(2)}, u32[]{:S(2)}) collective-permute-start(f32[32]{0:T(128)S(1)} %get-tuple-element.34), channel_id=1, source_target_pairs={{0,16},{4,20},{8,24},{12,28},{16,0},{20,4},{24,8},{28,12},{1,17},{... | collective-permute-start | bytes 392 | tf_op jit(solution)/shard_map/ppermute | solution.py:17
  487.9 7.3 %copy-start.7 = (bf16[1024,2048]{1,0:T(8,128)(2,1)S(1)}, bf16[1024,2048]{1,0:T(8,128)(2,1)}, u32[]{:S(2)}) copy-start(bf16[1024,2048]{1,0:T(8,128)(2,1)} %refs_4_.5) | copy-start | bytes 12582916
  492.4 3.4 copy-start.3
  511.6 6.3 %copy-start.16 = (f32[512,512]{1,0:T(8,128)S(1)}, f32[512,512]{1,0:T(8,128)}, u32[]{:S(2)}) copy-start(f32[512,512]{1,0:T(8,128)} %fusion.30) | copy-start | bytes 3145732
  515.7 2.2 copy-start.15
  515.7 2.2 copy-start.18
  515.7 3.2 copy-start.12
  515.7 3.2 copy-start.19
  515.7 3.1 copy-start.20
  515.8 3.1 copy-start.22
  533.9 2.9 copy-start.1
Sparse Core Ops, SparseCore 0:
  81.3 56.2 all-gather.5
  153.5 51.1 all-gather.3
  488.0 20.6 all-gather.7

commit v3 on v2

--- a/solution.py
+++ b/solution.py
@@ -17,17 +17,15 @@
     return lax.ppermute(value, axis, [(i, i ^ 1 << distance) for i in range(lax.axis_size(axis))])
 
 
-def project_kernel(count, added, place_ref, *refs):
+def project_kernel(count, place_ref, *refs):
     rows, weights = refs[:count], refs[count : 2 * count]
     total = jnp.dot(rows[0][...], weights[0][...], preferred_element_type=jnp.float32)
     for row, weight in zip(rows[1:], weights[1:]):
         total = total + jnp.dot(row[...], weight[...], preferred_element_type=jnp.float32)
-    if added:
-        total = total + refs[2 * count][...].astype(jnp.float32)
-    refs[-1][...] = total.astype(jnp.bfloat16)
+    refs[-1][...] = total.astype(refs[-1].dtype)
 
 
-def project(place, rows, blocks, extra=None):
+def project(place, rows, blocks, dtype):
     tok_rows = rows.shape[0]
     depth, width = blocks[0].shape
     tile = min(width, 256)
@@ -38,14 +36,11 @@
     ]
     in_specs += [pl.BlockSpec((depth, tile), lambda i, p: (0, i)) for _ in masks]
     operands = [rows] * len(blocks) + list(blocks)
-    if extra is not None:
-        in_specs.append(pl.BlockSpec((tok_rows, tile), lambda i, p: (0, i)))
-        operands.append(extra)
     flops = 2 * tok_rows * depth * len(blocks) * width
     moved = 2 * (rows.size + len(blocks) * depth * width + tok_rows * width)
     return pl.pallas_call(
-        functools.partial(project_kernel, len(blocks), extra is not None),
-        out_shape=jax.ShapeDtypeStruct((tok_rows, width), jnp.bfloat16),
+        functools.partial(project_kernel, len(blocks)),
+        out_shape=jax.ShapeDtypeStruct((tok_rows, width), dtype),
         grid_spec=pltpu.PrefetchScalarGridSpec(
             num_scalar_prefetch=1,
             grid=(width // tile,),
@@ -92,19 +87,20 @@
     kept = lax.dynamic_slice_in_dim(token_part, upper_half * depth, depth, 1)
     given = lax.dynamic_slice_in_dim(token_part, (1 - upper_half) * depth, depth, 1)
     taken = lax.ppermute(given, "ctx", across)
+    rows_other = lax.all_gather(taken, "tp", axis=0, tiled=True)
     rows_mine = lax.all_gather(kept, "tp", axis=0, tiled=True)
-    rows_other = lax.all_gather(taken, "tp", axis=0, tiled=True)
     gate_start, far_block = lax.optimization_barrier((w_gate, value_blocks[half // 2]))
     value_blocks[half // 2] = far_block
     gate_blocks = gather_blocks(gate_start, half)
     place = jnp.reshape(my_block % half, (1,)).astype(jnp.int32)
-    value_back = lax.ppermute(project(place, rows_other, value_blocks), "ctx", across)
-    gate_other, value_back = lax.optimization_barrier(
-        (project(place, rows_other, gate_blocks), value_back)
-    )
+    value_other = project(place, rows_other, value_blocks, jnp.bfloat16)
+    value_back = lax.ppermute(value_other, "ctx", across)
+    value_mine = project(place, rows_mine, value_blocks, jnp.float32)
+    gate_other = project(place, rows_other, gate_blocks, jnp.bfloat16)
     gate_back = lax.ppermute(gate_other, "ctx", across)
-    values_proj = project(place, rows_mine, value_blocks, value_back)
-    gates_proj = project(place, rows_mine, gate_blocks, gate_back)
+    gate_mine = project(place, rows_mine, gate_blocks, jnp.float32)
+    values_proj = (value_mine + value_back.astype(jnp.float32)).astype(jnp.bfloat16)
+    gates_proj = (gate_mine + gate_back.astype(jnp.float32)).astype(jnp.bfloat16)
     values3 = values_proj.reshape(tok_rows, head_count, HEAD_DIM)
     group_index = lax.axis_index("tp") * head_count // HPG
     write_vec = lax.dynamic_index_in_dim(state_proj[:, 0], group_index, 1, keepdims=False)

time: 550 us -> 533 us (0.969)
  waiting for transfers between devices: 378 us -> 366 us
    ppermute x1, waiting for transfers between devices: 68.9 us -> 0.01 us  [on_device(): value_back = lax.ppermute(value_other, 'ctx', across)]
    ppermute x12, waiting for transfers between devices: 241 us -> 297 us  [swapped(): lax.ppermute(value, axis, [(i, i ^ 1 << distance) for i in range(lax.axis...]
    convert_element_type x0 -> x2, other arithmetic: none -> 6.77 us  [the longest x1 4.5 us: on_device(): gates_proj.reshape(tok_rows, head_count, HEAD_DIM).astype(jnp.float32)]
  transfers between devices with their start and end apart: 19 -> 19, of which waited for: 8 -> 9; matrix products, arithmetic and copies ran while one was open for 6% -> 7% of each run, Pallas kernels for 7% -> 10%
where the time goes in v3:
time: 533 us; the launch traced here: 524 us
  waiting for transfers between devices  366 us (69%)
  Pallas kernels  50.9 us (10%)
  matrix products  31.5 us (6%)
  local copies, waits for them, and re-layouts  29.7 us (6%)
  starting transfers between devices  20.6 us (4%)
  between operations  13.5 us (3%)
  other arithmetic  11.8 us (2%)
    ppermute x12, waiting for transfers between devices, swapped(): lax.ppermute(value, axis, [(i, i ^ 1 << distance) for i in range(lax.axis...  297 us
    pallas_call x4, Pallas kernels, project(): pl.pallas_call(functools.partial(project_kernel, len(blocks)), out_shape=...  50.9 us
    ppermute x1, waiting for transfers between devices, on_device(): taken = lax.ppermute(given, 'ctx', across)  44.3 us
    all_to_all x1, waiting for transfers between devices, on_device(): token_part = lax.all_to_all(hidden_rows, 'tp', 0, 1, tiled=True)  24.3 us
    ppermute x12, starting transfers between devices, swapped(): lax.ppermute(value, axis, [(i, i ^ 1 << distance) for i in range(lax.axis...  16.6 us
    dot_general x1, matrix products, on_device(): jnp.einsum('hts,shp->thp', mixing, values3, preferred_element_type=jnp.fl...  15 us
    unnamed x47, local copies, waits for them, and re-layouts  13.4 us
  transfers between devices with their start and end apart: 19, of which 9 were waited for; matrix products, arithmetic and copies ran while one was open for 7% of the time, Pallas kernels for 10%

profile of v3, /device:TPU:17, one launch (start us, length us, event | category | flops | bytes accessed | tf_op | source)
XLA Modules:
  0.0 524.0 jit_solution(10778846170028386443)
XLA Ops:
  6.5 3.7 all-to-all-start
  10.4 24.3 %all-to-all-done = bf16[4,128,2048]{2,1,0:T(8,128)(2,1)S(1)} async-done(((bf16[4,128,2048]{2,1,0:T(8,128)(2,1)}), bf16[4,128,2048]{2,1,0:T(8,128)(2,1)S(1)}, u32[]{:S(2)}, u32[]{:S(2)}) %all-to-all-start) | async-done | bytes 2097184 | tf_op jit(solution)/shard_map/all_to_all | solution.py:85
  34.6 0.1 copy.52
  34.8 1.1 constant_dynamic-slice_fusion.2
  35.9 44.3 %collective-permute-done.3 = bf16[128,4096]{1,0:T(8,128)(2,1)S(1)} collective-permute-done((bf16[128,4096]{1,0:T(8,128)(2,1)S(1)}, bf16[128,4096]{1,0:T(8,128)(2,1)S(1)}, u32[]{:S(2)}, u32[]{:S(2)}) %collective-permute-start.3) | collective-permute-done | bytes 1048608 | tf_op jit(solution)/shard_map/ppermute | solution.py:89
  80.2 1.0 copy-done.16
  81.2 5.4 %collective-permute-start.1 = (bf16[1024,2048]{1,0:T(8,128)(2,1)}, bf16[1024,2048]{1,0:T(8,128)(2,1)}, u32[]{:S(2)}, u32[]{:S(2)}) collective-permute-start(bf16[1024,2048]{1,0:T(8,128)(2,1)} %refs_4_.3), channel_id=1, source_target_pairs={{0,8},{4,12},{8,0},{12,4},{16,24},{20,28},{24,16},{28,20},{1,9},{5... | collective-permute-start | bytes 12582920 | tf_op jit(solution)/shard_map/ppermute | solution.py:17
  86.6 0.8 collective-permute-start
  87.4 90.0 %collective-permute-done.1.refs_6_ = bf16[1024,2048]{1,0:T(8,128)(2,1)} collective-permute-done((bf16[1024,2048]{1,0:T(8,128)(2,1)}, bf16[1024,2048]{1,0:T(8,128)(2,1)}, u32[]{:S(2)}, u32[]{:S(2)}) %collective-permute-start.1) | collective-permute-done | bytes 4194336 | tf_op jit(solution)/shard_map/ppermute | solution.py:17
  177.4 1.1 collective-permute-start.2
  178.6 1.5 collective-permute-start.12
  180.1 1.2 reduce-window.6
  181.3 0.2 slice_reduce_fusion
  181.5 0.1 copy_bitcast_fusion.2
  181.6 4.0 collective-permute-done.2.refs_7_
  185.6 2.6 copy-done.4
  188.2 2.2 copy-done.6
  190.4 12.4 %shard_map.92 = bf16[512,2048]{1,0:T(8,128)(2,1)S(1)} custom-call(s32[1]{0:T(128)} %bitcast.1.place_ref, bf16[512,4096]{1,0:T(8,128)(2,1)S(1)} %copy-done.4, bf16[512,4096]{1,0:T(8,128)(2,1)S(1)} %copy-done.4, bf16[512,4096]{1,0:T(8,128)(2,1)S(1)} %copy-done.4, bf16[512,4096]{1,0:T(8,128)(2,1)S(1)} %copy-done.4, bf16[1024,2048]{1,0:T(8,128)(2,1)S(1)} %copy-done.6, ...), custom_call_target="tpu_custom_call" | custom-call | flops 8589934592 | bytes 23068672 | tf_op jit(solution)/shard_map/pallas_call | solution.py:41
  202.8 0.1 collective-permute-start.4
  202.9 0.2 slice_reduce_fusion.1
  203.1 0.4 collective-permute-start.6
  203.5 2.3 fusion.43
  205.8 0.2 collective-permute-start.11
  206.0 109.3 %collective-permute-done.12.refs_6_ = bf16[1024,2048]{1,0:T(8,128)(2,1)} collective-permute-done((bf16[1024,2048]{1,0:T(8,128)(2,1)}, bf16[1024,2048]{1,0:T(8,128)(2,1)}, u32[]{:S(2)}, u32[]{:S(2)}) %collective-permute-start.12) | collective-permute-done | bytes 4194336 | tf_op jit(solution)/shard_map/ppermute | solution.py:17
  315.3 0.9 collective-permute-start.13
  316.1 0.5 constant_dynamic-slice_fusion.1
  316.7 0.5 constant_dynamic-slice_fusion
  317.3 0.8 negate_exponential_fusion
  318.1 0.7 slice_bitcast_fusion.4
  318.9 2.2 copy-done.2
  321.1 2.2 copy-done.7
  323.3 12.4 %shard_map.91 = f32[512,2048]{1,0:T(8,128)S(1)} custom-call(s32[1]{0:T(128)} %bitcast.1.place_ref, bf16[512,4096]{1,0:T(8,128)(2,1)S(1)} %copy-done.2, bf16[512,4096]{1,0:T(8,128)(2,1)S(1)} %copy-done.2, bf16[512,4096]{1,0:T(8,128)(2,1)S(1)} %copy-done.2, bf16[512,4096]{1,0:T(8,128)(2,1)S(1)} %copy-done.2, bf16[1024,2048]{1,0:T(8,128)(2,1)S(1)} %copy-done.7, ...), custom_call_target="tpu_custom_call" | custom-call | flops 8589934592 | bytes 23068672 | tf_op jit(solution)/shard_map/pallas_call | solution.py:41
  335.7 2.3 add_convert_fusion.1
  338.0 2.5 copy.39
  340.5 4.9 fusion.44
  345.4 0.8 iota_compare_fusion
  346.2 1.3 fusion.31
  347.6 2.3 collective-permute-start.8
  349.9 0.1 dynamic-slice.2
  349.9 0.9 collective-permute-done.8
  350.8 0.6 negate_exponential_fusion.2
  351.4 0.1 dynamic-slice.3
  351.5 3.2 collective-permute-done.10
  354.7 0.6 fusion.41
  355.3 1.5 collective-permute-start.7
  356.9 13.0 %shard_map.94 = bf16[512,2048]{1,0:T(8,128)(2,1)S(1)} custom-call(s32[1]{0:T(128)} %bitcast.1.place_ref, bf16[512,4096]{1,0:T(8,128)(2,1)S(1)} %copy-done.5, bf16[512,4096]{1,0:T(8,128)(2,1)S(1)} %copy-done.5, bf16[512,4096]{1,0:T(8,128)(2,1)S(1)} %copy-done.5, bf16[512,4096]{1,0:T(8,128)(2,1)S(1)} %copy-done.5, bf16[1024,2048]{1,0:T(8,128)(2,1)} %refs_4_.5, ...), custom_call_target="tpu_custom_call" | custom-call | flops 8589934592 | bytes 23068672 | tf_op jit(solution)/shard_map/pallas_call | solution.py:41
  369.9 0.1 collective-permute-start.14
  370.0 2.8 fusion.14
  372.7 11.9 %collective-permute-done.7 = bf16[32,64,256]{2,1,0:T(8,128)(2,1)S(1)} collective-permute-done((bf16[32,64,256]{2,1,0:T(8,128)(2,1)S(1)}, bf16[32,64,256]{2,1,0:T(8,128)(2,1)S(1)}, u32[]{:S(2)}, u32[]{:S(2)}) %collective-permute-start.7) | collective-permute-done | bytes 1048608 | tf_op jit(solution)/shard_map/ppermute | solution.py:17
  384.7 0.3 convert_element_type.80
  384.9 0.2 select_convert_fusion.4
  385.1 2.5 collective-permute-start.9
  387.6 2.7 fusion.15
  390.3 78.1 %collective-permute-done.9 = bf16[8,64,256]{2,1,0:T(8,128)(2,1)} collective-permute-done((bf16[8,64,256]{2,1,0:T(8,128)(2,1)S(1)}, bf16[8,64,256]{2,1,0:T(8,128)(2,1)}, u32[]{:S(2)}, u32[]{:S(2)}) %collective-permute-start.9) | collective-permute-done | bytes 262176 | tf_op jit(solution)/shard_map/ppermute | solution.py:17
  468.4 2.2 copy-done.3
  470.6 13.0 %shard_map.93 = f32[512,2048]{1,0:T(8,128)S(1)} custom-call(s32[1]{0:T(128)} %bitcast.1.place_ref, bf16[512,4096]{1,0:T(8,128)(2,1)S(1)} %copy-done.3, bf16[512,4096]{1,0:T(8,128)(2,1)S(1)} %copy-done.3, bf16[512,4096]{1,0:T(8,128)(2,1)S(1)} %copy-done.3, bf16[512,4096]{1,0:T(8,128)(2,1)S(1)} %copy-done.3, bf16[1024,2048]{1,0:T(8,128)(2,1)} %refs_4_.5, ...), custom_call_target="tpu_custom_call" | custom-call | flops 8589934592 | bytes 23068672 | tf_op jit(solution)/shard_map/pallas_call | solution.py:41
  483.7 2.7 fusion.12
  486.4 4.5 fusion.11
  490.9 5.5 %copy.44 = f32[512,2048]{0,1:T(8,128)} copy(f32[512,2048]{1,0:T(8,128)} %fusion.11) | data formatting | bytes 8388608 | tf_op jit(solution)/shard_map/convert_element_type | solution.py:168
  496.5 2.1 fusion.13
  498.6 1.0 copy-done.8
  499.6 15.0 %multiply_reduce_fusion = (f32[512,32]{0,1:T(8,128)S(1)}, f32[512,32,64]{0,2,1:T(8,128)S(1)}) fusion(f32[512,32,64]{0,2,1:T(8,128)} %bitcast.71, bf16[512,32,64]{0,2,1:T(8,128)(2,1)S(1)} %bitcast.74, f32[32]{0:T(128)S(1)} %copy-done.22, f32[512,32]{0,1:T(8,128)S(1)} %copy-done.18, f32[512,32,64]{0,2,1:T(8,128)S(1)} %copy-done.8, ...), kind=kOutput, calls=%fused_computation.12 | convolution fusion | flops 1145028608 | bytes 29098112 | tf_op jit(solution)/shard_map/hts,shp->thp/dot_general | solution.py:117
  514.6 0.5 multiply_convert_fusion.4
  515.1 2.4 copy.45
  (67 shorter events, 0.5 us)
Async XLA Ops:
  6.5 173.5 %copy-start = (f32[512,32]{0,1:T(8,128)S(1)}, f32[512,32]{0,1:T(8,128)}, u32[]{:S(2)}) copy-start(f32[512,32]{0,1:T(8,128)} %param.13) | copy-start | bytes 196612
  6.5 28.1 %all-to-all-start = ((bf16[4,128,2048]{2,1,0:T(8,128)(2,1)}), bf16[4,128,2048]{2,1,0:T(8,128)(2,1)S(1)}, u32[]{:S(2)}, u32[]{:S(2)}) async-start(bf16[4,128,2048]{2,1,0:T(8,128)(2,1)} %bitcast.72), calls=%async_computation | async-start | bytes 4194304 | tf_op jit(solution)/shard_map/all_to_all | solution.py:85
  10.3 175.3 %all-gather.6.cloned.1.call-start = ((), (), s32[]{:S(2)}) async-start(), calls=%async_computation.2 | async-start | bytes 5242880 | tf_op jit(solution)/shard_map/all_gather | solution.py:90
  35.9 44.3 %collective-permute-start.3 = (bf16[128,4096]{1,0:T(8,128)(2,1)S(1)}, bf16[128,4096]{1,0:T(8,128)(2,1)S(1)}, u32[]{:S(2)}, u32[]{:S(2)}) collective-permute-start(bf16[128,4096]{1,0:T(8,128)(2,1)S(1)} %get-tuple-element.17), channel_id=1, source_target_pairs={{0,16},{4,20},{8,24},{12,28},{16,0},{20,4},{24,8},{28,12},{1,17},{... | collective-permute-start | bytes 3145736 | tf_op jit(solution)/shard_map/ppermute | solution.py:89
  80.2 1.0 copy-start.16
  81.2 237.7 %all-gather.4.cloned.1.call-start = ((), (), s32[]{:S(2)}) async-start(), calls=%async_computation.1 | async-start | bytes 5242880 | tf_op jit(solution)/shard_map/all_gather | solution.py:91
  81.2 96.2 %collective-permute-start.1 = (bf16[1024,2048]{1,0:T(8,128)(2,1)}, bf16[1024,2048]{1,0:T(8,128)(2,1)}, u32[]{:S(2)}, u32[]{:S(2)}) collective-permute-start(bf16[1024,2048]{1,0:T(8,128)(2,1)} %refs_4_.3), channel_id=1, source_target_pairs={{0,8},{4,12},{8,0},{12,4},{16,24},{20,28},{24,16},{28,20},{1,9},{5... | collective-permute-start | bytes 12582920 | tf_op jit(solution)/shard_map/ppermute | solution.py:17
  86.6 94.9 %collective-permute-start = (bf16[1024,2048]{1,0:T(8,128)(2,1)}, bf16[1024,2048]{1,0:T(8,128)(2,1)}, u32[]{:S(2)}, u32[]{:S(2)}) collective-permute-start(bf16[1024,2048]{1,0:T(8,128)(2,1)} %refs_4_.3), channel_id=1, source_target_pairs={{0,4},{4,0},{8,12},{12,8},{16,20},{20,16},{24,28},{28,24},{1,5},{5... | collective-permute-start | bytes 12582920 | tf_op jit(solution)/shard_map/ppermute | solution.py:17
  177.4 8.2 %collective-permute-start.2 = (bf16[1024,2048]{1,0:T(8,128)(2,1)}, bf16[1024,2048]{1,0:T(8,128)(2,1)}, u32[]{:S(2)}, u32[]{:S(2)}) collective-permute-start(bf16[1024,2048]{1,0:T(8,128)(2,1)} %collective-permute-done.1.refs_6_), channel_id=1, source_target_pairs={{0,4},{4,0},{8,12},{12,8},{16,20},{20,16},{24,28},{28,24},{1,5},{5... | collective-permute-start | bytes 12582920 | tf_op jit(solution)/shard_map/ppermute | solution.py:17
  178.5 317.9 %all-gather.8.cloned.1.call-start = ((), (), s32[]{:S(2)}) async-start(), calls=%async_computation.3 | async-start | bytes 1310720 | tf_op jit(solution)/shard_map/all_gather | solution.py:141
  178.6 136.7 %collective-permute-start.12 = (bf16[1024,2048]{1,0:T(8,128)(2,1)}, bf16[1024,2048]{1,0:T(8,128)(2,1)}, u32[]{:S(2)}, u32[]{:S(2)}) collective-permute-start(bf16[1024,2048]{1,0:T(8,128)(2,1)} %refs_4_.5), channel_id=1, source_target_pairs={{0,8},{4,12},{8,0},{12,4},{16,24},{20,28},{24,16},{28,20},{1,9},{5... | collective-permute-start | bytes 12582920 | tf_op jit(solution)/shard_map/ppermute | solution.py:17
  185.6 2.6 copy-start.4
  188.2 2.2 copy-start.6
  202.8 115.3 %copy-start.17 = (f32[6,512,32]{1,2,0:T(8,128)S(1)}, f32[6,512,32]{1,2,0:T(8,128)}, u32[]{:S(2)}) copy-start(f32[6,512,32]{1,2,0:T(8,128)} %param.14) | copy-start | bytes 1179652
  202.8 132.9 %collective-permute-start.4 = (bf16[512,2048]{1,0:T(8,128)(2,1)S(1)}, bf16[512,2048]{1,0:T(8,128)(2,1)}, u32[]{:S(2)}, u32[]{:S(2)}) collective-permute-start(bf16[512,2048]{1,0:T(8,128)(2,1)S(1)} %shard_map.92), channel_id=1, source_target_pairs={{0,16},{4,20},{8,24},{12,28},{16,0},{20,4},{24,8},{28,12},{1,17},{... | collective-permute-start | bytes 6291464 | tf_op jit(solution)/shard_map/ppermute | solution.py:97
  203.1 144.5 %collective-permute-start.6 = (f32[32]{0:T(128)S(1)}, f32[32]{0:T(128)S(1)}, u32[]{:S(2)}, u32[]{:S(2)}) collective-permute-start(f32[32]{0:T(128)S(1)} %slice_reduce_fusion.1), channel_id=1, source_target_pairs={{0,4},{4,0},{8,12},{12,8},{16,20},{20,16},{24,28},{28,24},{1,5},{5... | collective-permute-start | bytes 392 | tf_op jit(solution)/shard_map/ppermute | solution.py:17
  205.8 151.1 %collective-permute-start.11 = (bf16[1024,2048]{1,0:T(8,128)(2,1)}, bf16[1024,2048]{1,0:T(8,128)(2,1)}, u32[]{:S(2)}, u32[]{:S(2)}) collective-permute-start(bf16[1024,2048]{1,0:T(8,128)(2,1)} %refs_4_.5), channel_id=1, source_target_pairs={{0,4},{4,0},{8,12},{12,8},{16,20},{20,16},{24,28},{28,24},{1,5},{5... | collective-permute-start | bytes 12582920 | tf_op jit(solution)/shard_map/ppermute | solution.py:17
  315.3 41.6 %collective-permute-start.13 = (bf16[1024,2048]{1,0:T(8,128)(2,1)}, bf16[1024,2048]{1,0:T(8,128)(2,1)}, u32[]{:S(2)}, u32[]{:S(2)}) collective-permute-start(bf16[1024,2048]{1,0:T(8,128)(2,1)} %collective-permute-done.12.refs_6_), channel_id=1, source_target_pairs={{0,4},{4,0},{8,12},{12,8},{16,20},{20,16},{24,28},{28,24},{1,5},{5... | collective-permute-start | bytes 12582920 | tf_op jit(solution)/shard_map/ppermute | solution.py:17
  317.3 1.6 copy-start.12
  318.9 2.2 copy-start.2
  321.1 2.2 copy-start.7
  340.5 5.7 %copy-start.13 = (bf16[512,1,1,256]{3,2,1,0:T(2,128)(2,1)S(1)}, bf16[512,1,1,256]{3,2,1,0:T(2,128)(2,1)}, u32[]{:S(2)}) copy-start(bf16[512,1,1,256]{3,2,1,0:T(2,128)(2,1)} %copy-done.12) | copy-start | bytes 786436
  340.5 7.0 %copy-start.21 = (f32[2048]{0:T(1024)S(1)}, f32[2048]{0:T(1024)}, u32[]{:S(2)}) copy-start(f32[2048]{0:T(1024)} %param.17) | copy-start | bytes 24580
  345.4 9.3 %collective-permute-start.5 = (bf16[32,64,256]{2,1,0:T(8,128)(2,1)}, bf16[32,64,256]{2,1,0:T(8,128)(2,1)S(1)}, u32[]{:S(2)}, u32[]{:S(2)}) collective-permute-start(bf16[32,64,256]{2,1,0:T(8,128)(2,1)} %get-tuple-element.33), channel_id=1, source_target_pairs={{0,4},{4,0},{8,12},{12,8},{16,20},{20,16},{24,28},{28,24},{1,5},{5... | collective-permute-start | bytes 3145736 | tf_op jit(solution)/shard_map/ppermute | solution.py:17
  347.6 9.3 %copy-start.5 = (bf16[512,4096]{1,0:T(8,128)(2,1)S(1)}, bf16[512,4096]{1,0:T(8,128)(2,1)}, u32[]{:S(2)}) copy-start(bf16[512,4096]{1,0:T(8,128)(2,1)} %all-gather.6.cloned.1.call-done.refs_0_.refs_1_.refs_2_.refs_3_) | copy-start | bytes 12582916
  347.6 3.2 collective-permute-start.8
  351.4 3.3 collective-permute-start.10
  355.3 14.6 %copy-start.11 = (f32[32,64,256]{2,1,0:T(8,128)S(1)}, f32[32,64,256]{2,1,0:T(8,128)}, u32[]{:S(2)}) copy-start(f32[32,64,256]{2,1,0:T(8,128)} %param.15) | copy-start | bytes 6291460
  355.3 29.3 %collective-permute-start.7 = (bf16[32,64,256]{2,1,0:T(8,128)(2,1)S(1)}, bf16[32,64,256]{2,1,0:T(8,128)(2,1)S(1)}, u32[]{:S(2)}, u32[]{:S(2)}) collective-permute-start(bf16[32,64,256]{2,1,0:T(8,128)(2,1)S(1)} %get-tuple-element.13), channel_id=1, source_target_pairs={{0,8},{4,12},{8,0},{12,4},{16,24},{20,28},{24,16},{28,20},{1,9},{5... | collective-permute-start | bytes 3145736 | tf_op jit(solution)/shard_map/ppermute | solution.py:17
  369.9 116.5 %collective-permute-start.14 = (bf16[512,2048]{1,0:T(8,128)(2,1)S(1)}, bf16[512,2048]{1,0:T(8,128)(2,1)}, u32[]{:S(2)}, u32[]{:S(2)}) collective-permute-start(bf16[512,2048]{1,0:T(8,128)(2,1)S(1)} %shard_map.94), channel_id=1, source_target_pairs={{0,16},{4,20},{8,24},{12,28},{16,0},{20,4},{24,8},{28,12},{1,17},{... | collective-permute-start | bytes 6291464 | tf_op jit(solution)/shard_map/ppermute | solution.py:100
  384.7 5.7 %copy-start.9 = (bf16[32,64,256]{2,1,0:T(8,128)(2,1)}, bf16[32,64,256]{2,1,0:T(8,128)(2,1)S(1)}, u32[]{:S(2)}) copy-start(bf16[32,64,256]{2,1,0:T(8,128)(2,1)S(1)} %collective-permute-done.7) | copy-start | bytes 3145732
  385.1 83.3 %collective-permute-start.9 = (bf16[8,64,256]{2,1,0:T(8,128)(2,1)S(1)}, bf16[8,64,256]{2,1,0:T(8,128)(2,1)}, u32[]{:S(2)}, u32[]{:S(2)}) collective-permute-start(bf16[8,64,256]{2,1,0:T(8,128)(2,1)S(1)} %select_convert_fusion.4), channel_id=1, source_target_pairs={{0,16},{4,20},{8,24},{12,28},{16,0},{20,4},{24,8},{28,12},{1,17},{... | collective-permute-start | bytes 786440 | tf_op jit(solution)/shard_map/ppermute | solution.py:17
  468.4 2.2 copy-start.3
  470.6 13.0 %copy-start.10 = (bf16[32,64,256]{2,1,0:T(8,128)(2,1)S(1)}, bf16[32,64,256]{2,1,0:T(8,128)(2,1)}, u32[]{:S(2)}) copy-start(bf16[32,64,256]{2,1,0:T(8,128)(2,1)} %copy-done.9) | copy-start | bytes 3145732
  490.9 7.7 %copy-start.15 = (f32[512,512]{1,0:T(8,128)S(1)}, f32[512,512]{1,0:T(8,128)}, u32[]{:S(2)}) copy-start(f32[512,512]{1,0:T(8,128)} %fusion.31) | copy-start | bytes 3145732
  496.4 2.2 copy-start.14
  496.4 2.2 copy-start.18
  496.4 3.2 copy-start.8
  496.4 3.2 copy-start.19
  496.4 3.1 copy-start.20
  496.4 3.1 copy-start.22
  514.6 2.9 copy-start.1
Sparse Core Ops, SparseCore 0:
  81.3 56.1 all-gather.5
  178.6 51.9 all-gather.3
  468.6 23.4 all-gather.7

commit v4 on v3

--- a/solution.py
+++ b/solution.py
@@ -81,7 +81,13 @@
     upper_half = my_block // half
     groups = [list(range(half)), list(range(half, ctx_size))]
     across = [(i, (i + half) % ctx_size) for i in range(ctx_size)]
-    value_blocks = gather_blocks(w_value, half)
+    chunks = 2
+    width = w_value.shape[1] // chunks
+    moved = {}
+    for part, weight in (("value", w_value), ("gate", w_gate)):
+        for chunk in range(chunks):
+            piece = lax.slice_in_dim(weight, chunk * width, (chunk + 1) * width, axis=1)
+            moved[part, chunk] = gather_blocks(piece, half)
     token_part = lax.all_to_all(hidden_rows, "tp", 0, 1, tiled=True)
     depth = token_part.shape[1] // 2
     kept = lax.dynamic_slice_in_dim(token_part, upper_half * depth, depth, 1)
@@ -89,18 +95,14 @@
     taken = lax.ppermute(given, "ctx", across)
     rows_other = lax.all_gather(taken, "tp", axis=0, tiled=True)
     rows_mine = lax.all_gather(kept, "tp", axis=0, tiled=True)
-    gate_start, far_block = lax.optimization_barrier((w_gate, value_blocks[half // 2]))
-    value_blocks[half // 2] = far_block
-    gate_blocks = gather_blocks(gate_start, half)
     place = jnp.reshape(my_block % half, (1,)).astype(jnp.int32)
-    value_other = project(place, rows_other, value_blocks, jnp.bfloat16)
-    value_back = lax.ppermute(value_other, "ctx", across)
-    value_mine = project(place, rows_mine, value_blocks, jnp.float32)
-    gate_other = project(place, rows_other, gate_blocks, jnp.bfloat16)
-    gate_back = lax.ppermute(gate_other, "ctx", across)
-    gate_mine = project(place, rows_mine, gate_blocks, jnp.float32)
-    values_proj = (value_mine + value_back.astype(jnp.float32)).astype(jnp.bfloat16)
-    gates_proj = (gate_mine + gate_back.astype(jnp.float32)).astype(jnp.bfloat16)
+    sums = {}
+    for (part, chunk), blocks in moved.items():
+        back = lax.ppermute(project(place, rows_other, blocks, jnp.bfloat16), "ctx", across)
+        mine = project(place, rows_mine, blocks, jnp.float32)
+        sums[part, chunk] = (mine + back.astype(jnp.float32)).astype(jnp.bfloat16)
+    values_proj = jnp.concatenate([sums["value", chunk] for chunk in range(chunks)], axis=1)
+    gates_proj = jnp.concatenate([sums["gate", chunk] for chunk in range(chunks)], axis=1)
     values3 = values_proj.reshape(tok_rows, head_count, HEAD_DIM)
     group_index = lax.axis_index("tp") * head_count // HPG
     write_vec = lax.dynamic_index_in_dim(state_proj[:, 0], group_index, 1, keepdims=False)

time: 533 us -> 529 us (level); the launches traced: 524 us -> 526 us
  waiting for transfers between devices: 366 us -> 333 us
  starting transfers between devices: 20.6 us -> 33.6 us
  Pallas kernels: 50.9 us -> 63 us
    ppermute x12 -> x18, waiting for transfers between devices: 297 us -> 162 us  [swapped(): lax.ppermute(value, axis, [(i, i ^ 1 << distance) for i in range(lax.axis...]
    ppermute x2 -> x4, waiting for transfers between devices: 0.01 us -> 96.5 us  [on_device(): lax.ppermute(project(place, rows_other, blocks, jnp.bfloat16), 'ctx', acr...]
    pallas_call x4 -> x8, Pallas kernels: 50.9 us -> 63 us  [project(): pl.pallas_call(functools.partial(project_kernel, len(blocks)), out_shape=...]
    unnamed x47 -> x61, local copies, waits for them, and re-layouts: 13.4 us -> 5.89 us
    ppermute x12 -> x18, starting transfers between devices: 16.6 us -> 24.1 us  [swapped(): lax.ppermute(value, axis, [(i, i ^ 1 << distance) for i in range(lax.axis...]
    slice x1 -> x3, local copies, waits for them, and re-layouts: 0.17 us -> 6.77 us  [the longest x2 6.61 us: on_device(): piece = lax.slice_in_dim(weight, chunk * width, (chunk + 1) * width, axis=1)]
    ppermute x2 -> x4, starting transfers between devices: 0.14 us -> 5.65 us  [on_device(): lax.ppermute(project(place, rows_other, blocks, jnp.bfloat16), 'ctx', acr...]
  transfers between devices with their start and end apart: 19 -> 27, of which waited for: 9 -> 11; matrix products, arithmetic and copies ran while one was open for 7% -> 12% of each run, Pallas kernels for 10% -> 12%
where the time goes in v4:
time: 529 us; the launch traced here: 526 us
  waiting for transfers between devices  333 us (63%)
  Pallas kernels  63 us (12%)
  local copies, waits for them, and re-layouts  34.8 us (7%)
  starting transfers between devices  33.6 us (6%)
  matrix products  32.8 us (6%)
  other arithmetic  15.7 us (3%)
  between operations  13.6 us (3%)
    ppermute x18, waiting for transfers between devices, swapped(): lax.ppermute(value, axis, [(i, i ^ 1 << distance) for i in range(lax.axis...  162 us
    ppermute x4, waiting for transfers between devices, on_device(): lax.ppermute(project(place, rows_other, blocks, jnp.bfloat16), 'ctx', acr...  96.5 us
    pallas_call x8, Pallas kernels, project(): pl.pallas_call(functools.partial(project_kernel, len(blocks)), out_shape=...  63 us
    ppermute x1, waiting for transfers between devices, on_device(): taken = lax.ppermute(given, 'ctx', across)  44.3 us
    all_to_all x1, waiting for transfers between devices, on_device(): token_part = lax.all_to_all(hidden_rows, 'tp', 0, 1, tiled=True)  24.3 us
    ppermute x18, starting transfers between devices, swapped(): lax.ppermute(value, axis, [(i, i ^ 1 << distance) for i in range(lax.axis...  24.1 us
    dot_general x4, matrix products, on_device(): lax.dot_general(read_vec, state, (((1,), (2,)), ((), ())), preferred_elem...  14.7 us
    dot_general x1, matrix products, on_device(): jnp.einsum('hts,shp->thp', mixing, values3, preferred_element_type=jnp.fl...  12.3 us
  transfers between devices with their start and end apart: 27, of which 11 were waited for; matrix products, arithmetic and copies ran while one was open for 12% of the time, Pallas kernels for 12%

profile of v4, /device:TPU:17, one launch (start us, length us, event | category | flops | bytes accessed | tf_op | source)
XLA Modules:
  0.0 526.4 jit_solution(18368850117897177118)
XLA Ops:
  6.5 3.7 all-to-all-start
  10.4 24.3 %all-to-all-done = bf16[4,128,2048]{2,1,0:T(8,128)(2,1)S(1)} async-done(((bf16[4,128,2048]{2,1,0:T(8,128)(2,1)}), bf16[4,128,2048]{2,1,0:T(8,128)(2,1)S(1)}, u32[]{:S(2)}, u32[]{:S(2)}) %all-to-all-start) | async-done | bytes 2097184 | tf_op jit(solution)/shard_map/all_to_all | solution.py:91
  34.6 1.3 copy-done.4
  36.0 1.8 copy.52
  37.8 1.2 constant_dynamic-slice_fusion.2
  39.0 44.3 %collective-permute-done.3 = bf16[128,4096]{1,0:T(8,128)(2,1)S(1)} collective-permute-done((bf16[128,4096]{1,0:T(8,128)(2,1)S(1)}, bf16[128,4096]{1,0:T(8,128)(2,1)S(1)}, u32[]{:S(2)}, u32[]{:S(2)}) %collective-permute-start.3) | collective-permute-done | bytes 1048608 | tf_op jit(solution)/shard_map/ppermute | solution.py:95
  83.2 1.0 copy-done.11
  84.3 0.7 all-gather.4.cloned.1.call-update
  85.0 4.8 fusion.42
  89.9 5.3 %collective-permute-start.6 = (bf16[1024,1024]{1,0:T(8,128)(2,1)}, bf16[1024,1024]{1,0:T(8,128)(2,1)}, u32[]{:S(2)}, u32[]{:S(2)}) collective-permute-start(bf16[1024,1024]{1,0:T(8,128)(2,1)} %get-tuple-element.14.refs_4_), channel_id=1, source_target_pairs={{0,8},{4,12},{8,0},{12,4},{16,24},{20,28},{24,16},{28,20},{1,9},{5... | collective-permute-start | bytes 6291464 | tf_op jit(solution)/shard_map/ppermute | solution.py:17
  95.3 0.8 collective-permute-start.5
  96.0 1.8 fusion.41
  97.8 1.7 collective-permute-start.20
  99.5 1.2 reduce-window.6
  101.8 2.3 fusion.43
  105.2 35.9 %collective-permute-done.6.refs_6_ = bf16[1024,1024]{1,0:T(8,128)(2,1)} collective-permute-done((bf16[1024,1024]{1,0:T(8,128)(2,1)}, bf16[1024,1024]{1,0:T(8,128)(2,1)}, u32[]{:S(2)}, u32[]{:S(2)}) %collective-permute-start.6) | collective-permute-done | bytes 2097184 | tf_op jit(solution)/shard_map/ppermute | solution.py:17
  141.1 1.7 collective-permute-start.7
  143.4 1.7 collective-permute-start.12
  145.2 85.8 %collective-permute-done.12 = f32[32]{0:T(128)S(1)} collective-permute-done((f32[32]{0:T(128)S(1)}, f32[32]{0:T(128)S(1)}, u32[]{:S(2)}, u32[]{:S(2)}) %collective-permute-start.12) | collective-permute-done | bytes 160 | tf_op jit(solution)/shard_map/ppermute | solution.py:17
  231.5 0.8 mul.230
  232.3 2.5 collective-permute-done.14
  234.9 2.2 collective-permute-start
  237.1 0.8 iota_compare_fusion
  237.9 1.4 negate_exponential_fusion
  239.3 1.7 slice_bitcast_fusion.4
  241.0 0.8 fusion.31
  241.8 1.3 fusion.29
  244.4 1.5 collective-permute-start.16
  245.8 2.8 fusion.12
  248.7 0.8 collective-permute-start.19
  249.5 2.2 copy-done.2
  251.7 7.0 %shard_map.94 = bf16[512,1024]{1,0:T(8,128)(2,1)S(1)} custom-call(s32[1]{0:T(128)} %bitcast.1.place_ref, bf16[512,4096]{1,0:T(8,128)(2,1)S(1)} %copy-done.2, bf16[512,4096]{1,0:T(8,128)(2,1)S(1)} %copy-done.2, bf16[512,4096]{1,0:T(8,128)(2,1)S(1)} %copy-done.2, bf16[512,4096]{1,0:T(8,128)(2,1)S(1)} %copy-done.2, ...), custom_call_target="tpu_custom_call" | custom-call | flops 4294967296 | bytes 13631488 | tf_op jit(solution)/shard_map/pallas_call | solution.py:41
  258.9 7.8 %shard_map.92 = bf16[512,1024]{1,0:T(8,128)(2,1)} custom-call(s32[1]{0:T(128)} %bitcast.1.place_ref, bf16[512,4096]{1,0:T(8,128)(2,1)S(1)} %copy-done.2, bf16[512,4096]{1,0:T(8,128)(2,1)S(1)} %copy-done.2, bf16[512,4096]{1,0:T(8,128)(2,1)S(1)} %copy-done.2, bf16[512,4096]{1,0:T(8,128)(2,1)S(1)} %copy-done.2, bf16[1024,1024]{1,0:T(8,128)(2,1)} %get-tuple-element.13.refs_4_, ...), custom_call_target="tpu_custom_call" | custom-call | flops 4294967296 | bytes 13631488 | tf_op jit(solution)/shard_map/pallas_call | solution.py:41
  266.7 2.3 collective-permute-start.4
  269.0 8.5 %shard_map.93 = f32[512,1024]{1,0:T(8,128)S(1)} custom-call(s32[1]{0:T(128)} %bitcast.1.place_ref, bf16[512,4096]{1,0:T(8,128)(2,1)} %all-gather.4.cloned.1.call-done.refs_0_.refs_1_.refs_2_.refs_3_, bf16[512,4096]{1,0:T(8,128)(2,1)} %all-gather.4.cloned.1.call-done.refs_0_.refs_1_.refs_2_.refs_3_, ...), custom_call_target="tpu_custom_call" | custom-call | flops 4294967296 | bytes 13631488 | tf_op jit(solution)/shard_map/pallas_call | solution.py:41
  277.6 8.6 %shard_map.91 = f32[512,1024]{1,0:T(8,128)S(1)} custom-call(s32[1]{0:T(128)} %bitcast.1.place_ref, bf16[512,4096]{1,0:T(8,128)(2,1)} %all-gather.4.cloned.1.call-done.refs_0_.refs_1_.refs_2_.refs_3_, bf16[512,4096]{1,0:T(8,128)(2,1)} %all-gather.4.cloned.1.call-done.refs_0_.refs_1_.refs_2_.refs_3_, ...), custom_call_target="tpu_custom_call" | custom-call | flops 4294967296 | bytes 13631488 | tf_op jit(solution)/shard_map/pallas_call | solution.py:41
  286.1 34.7 %collective-permute-done.16.refs_6_ = bf16[1024,1024]{1,0:T(8,128)(2,1)} collective-permute-done((bf16[1024,1024]{1,0:T(8,128)(2,1)S(1)}, bf16[1024,1024]{1,0:T(8,128)(2,1)}, u32[]{:S(2)}, u32[]{:S(2)}) %collective-permute-start.16) | collective-permute-done | bytes 2097184 | tf_op jit(solution)/shard_map/ppermute | solution.py:17
  320.9 1.4 collective-permute-start.15
  322.2 1.6 add_convert_fusion.2
  323.8 25.0 %collective-permute-done.4 = bf16[512,1024]{1,0:T(8,128)(2,1)} collective-permute-done((bf16[512,1024]{1,0:T(8,128)(2,1)}, bf16[512,1024]{1,0:T(8,128)(2,1)}, u32[]{:S(2)}, u32[]{:S(2)}) %collective-permute-start.4) | collective-permute-done | bytes 1048608 | tf_op jit(solution)/shard_map/ppermute | solution.py:101
  348.8 1.6 add_convert_fusion.3
  350.3 1.5 pad_maximum_fusion
  351.8 4.0 copy.39
  355.9 4.6 fusion.44
  360.4 1.1 collective-permute-start.9
  361.5 8.9 %shard_map.97 = f32[512,1024]{1,0:T(8,128)S(1)} custom-call(s32[1]{0:T(128)} %bitcast.1.place_ref, bf16[512,4096]{1,0:T(8,128)(2,1)} %all-gather.4.cloned.1.call-done.refs_0_.refs_1_.refs_2_.refs_3_, bf16[512,4096]{1,0:T(8,128)(2,1)} %all-gather.4.cloned.1.call-done.refs_0_.refs_1_.refs_2_.refs_3_, ...), custom_call_target="tpu_custom_call" | custom-call | flops 4294967296 | bytes 13631488 | tf_op jit(solution)/shard_map/pallas_call | solution.py:41
  370.4 7.1 %shard_map.98 = bf16[512,1024]{1,0:T(8,128)(2,1)S(1)} custom-call(s32[1]{0:T(128)} %bitcast.1.place_ref, bf16[512,4096]{1,0:T(8,128)(2,1)S(1)} %copy-done.3, bf16[512,4096]{1,0:T(8,128)(2,1)S(1)} %copy-done.3, bf16[512,4096]{1,0:T(8,128)(2,1)S(1)} %copy-done.3, bf16[512,4096]{1,0:T(8,128)(2,1)S(1)} %copy-done.3, ...), custom_call_target="tpu_custom_call" | custom-call | flops 4294967296 | bytes 13631488 | tf_op jit(solution)/shard_map/pallas_call | solution.py:41
  377.5 3.2 collective-permute-start.22
  380.7 6.9 %shard_map.96 = bf16[512,1024]{1,0:T(8,128)(2,1)S(1)} custom-call(s32[1]{0:T(128)} %bitcast.1.place_ref, bf16[512,4096]{1,0:T(8,128)(2,1)S(1)} %copy-done.3, bf16[512,4096]{1,0:T(8,128)(2,1)S(1)} %copy-done.3, bf16[512,4096]{1,0:T(8,128)(2,1)S(1)} %copy-done.3, bf16[512,4096]{1,0:T(8,128)(2,1)S(1)} %copy-done.3, ...), custom_call_target="tpu_custom_call" | custom-call | flops 4294967296 | bytes 13631488 | tf_op jit(solution)/shard_map/pallas_call | solution.py:41
  388.3 2.4 collective-permute-start.11
  390.7 8.2 %shard_map.95 = f32[512,1024]{1,0:T(8,128)S(1)} custom-call(s32[1]{0:T(128)} %bitcast.1.place_ref, bf16[512,4096]{1,0:T(8,128)(2,1)} %all-gather.4.cloned.1.call-done.refs_0_.refs_1_.refs_2_.refs_3_, bf16[512,4096]{1,0:T(8,128)(2,1)} %all-gather.4.cloned.1.call-done.refs_0_.refs_1_.refs_2_.refs_3_, ...), custom_call_target="tpu_custom_call" | custom-call | flops 4294967296 | bytes 13631488 | tf_op jit(solution)/shard_map/pallas_call | solution.py:41
  398.9 49.4 %collective-permute-done.22 = bf16[512,1024]{1,0:T(8,128)(2,1)S(1)} collective-permute-done((bf16[512,1024]{1,0:T(8,128)(2,1)S(1)}, bf16[512,1024]{1,0:T(8,128)(2,1)S(1)}, u32[]{:S(2)}, u32[]{:S(2)}) %collective-permute-start.22) | collective-permute-done | bytes 1048608 | tf_op jit(solution)/shard_map/ppermute | solution.py:101
  448.6 22.1 %collective-permute-done.18 = bf16[512,1024]{1,0:T(8,128)(2,1)S(1)} collective-permute-done((bf16[512,1024]{1,0:T(8,128)(2,1)S(1)}, bf16[512,1024]{1,0:T(8,128)(2,1)S(1)}, u32[]{:S(2)}, u32[]{:S(2)}) %collective-permute-start.18) | collective-permute-done | bytes 1048608 | tf_op jit(solution)/shard_map/ppermute | solution.py:101
  471.8 0.9 select_convert_fusion.4
  472.7 3.1 collective-permute-start.13
  475.8 2.5 maximum_convert_fusion
  478.3 5.5 %copy.44 = f32[512,2048]{0,1:T(8,128)} copy(f32[512,2048]{1,0:T(8,128)} %maximum_convert_fusion) | data formatting | bytes 8388608 | tf_op jit(solution)/shard_map/convert_element_type | solution.py:170
  483.8 2.8 collective-permute-done.13
  486.6 12.3 %fusion = f32[32,64,512]{2,1,0:T(8,128)} fusion(bf16[512,32,64]{0,2,1:T(8,128)(2,1)S(1)} %bitcast.76, f32[512,512]{1,0:T(8,128)} %fusion.29, f32[32,512]{1,0:T(8,128)S(1)} %get-tuple-element.27, pred[512,512]{1,0:T(8,128)(4,1)} %iota_compare_fusion), kind=kOutput, calls=%fused_computation.2 | convolution fusion | flops 1124073472 | bytes 7667712 | tf_op jit(solution)/shard_map/hts,shp->thp/dot_general | solution.py:119
  498.9 2.7 fusion.13
  501.6 5.3 %all-gather.8.cloned.1.call-done = bf16[32,64,256]{2,1,0:T(8,128)(2,1)} async-done(((bf16[8,64,256]{2,1,0:T(8,128)(2,1)}), bf16[32,64,256]{2,1,0:T(8,128)(2,1)}) %all-gather.8.cloned.1.call-update) | async-done | bytes 1048592 | tf_op jit(solution)/shard_map/all_gather | solution.py:143
  506.9 2.1 fusion.11
  509.7 7.1 %multiply_reduce_fusion = (f32[512,32]{0,1:T(8,128)S(1)}, f32[512,32,64]{0,2,1:T(8,128)S(1)}) fusion(f32[512,32,64]{0,2,1:T(8,128)} %bitcast.73, bf16[512,32,64]{0,2,1:T(8,128)(2,1)S(1)} %bitcast.77, f32[32]{0:T(128)S(1)} %copy-done.29, f32[512,32]{0,1:T(8,128)S(1)} %copy-done.13, f32[512,32,64]{0,2,1:T(8,128)S(1)} %copy-done.5, ...), kind=kOutput, calls=%fused_computation.12 | convolution fusion | flops 559923200 | bytes 29032704 | tf_op jit(solution)/shard_map/dot_general | solution.py:160
  517.5 2.4 copy.45
  (107 shorter events, 8.4 us)
Async XLA Ops:
  6.5 93.0 %copy-start = (f32[512,32]{0,1:T(8,128)S(1)}, f32[512,32]{0,1:T(8,128)}, u32[]{:S(2)}) copy-start(f32[512,32]{0,1:T(8,128)} %param.13) | copy-start | bytes 196612
  6.5 28.1 %all-to-all-start = ((bf16[4,128,2048]{2,1,0:T(8,128)(2,1)}), bf16[4,128,2048]{2,1,0:T(8,128)(2,1)S(1)}, u32[]{:S(2)}, u32[]{:S(2)}) async-start(bf16[4,128,2048]{2,1,0:T(8,128)(2,1)} %bitcast.74), calls=%async_computation | async-start | bytes 4194304 | tf_op jit(solution)/shard_map/all_to_all | solution.py:91
  10.3 239.2 %all-gather.6.cloned.1.call-start = ((), (), s32[]{:S(2)}) async-start(), calls=%async_computation.2 | async-start | bytes 5242880 | tf_op jit(solution)/shard_map/all_gather | solution.py:96
  34.6 1.3 copy-start.4
  39.0 44.3 %collective-permute-start.3 = (bf16[128,4096]{1,0:T(8,128)(2,1)S(1)}, bf16[128,4096]{1,0:T(8,128)(2,1)S(1)}, u32[]{:S(2)}, u32[]{:S(2)}) collective-permute-start(bf16[128,4096]{1,0:T(8,128)(2,1)S(1)} %get-tuple-element.17), channel_id=1, source_target_pairs={{0,16},{4,20},{8,24},{12,28},{16,0},{20,4},{24,8},{28,12},{1,17},{... | collective-permute-start | bytes 3145736 | tf_op jit(solution)/shard_map/ppermute | solution.py:95
  83.2 1.0 copy-start.11
  84.2 184.8 %all-gather.4.cloned.1.call-start = ((), (), s32[]{:S(2)}) async-start(), calls=%async_computation.1 | async-start | bytes 5242880 | tf_op jit(solution)/shard_map/all_gather | solution.py:97
  85.0 421.9 %all-gather.8.cloned.1.call-start = ((), (), s32[]{:S(2)}) async-start(), calls=%async_computation.3 | async-start | bytes 1310720 | tf_op jit(solution)/shard_map/all_gather | solution.py:143
  85.0 11.0 %copy-start.6 = (bf16[1024,2048]{1,0:T(8,128)(2,1)S(1)}, bf16[1024,2048]{1,0:T(8,128)(2,1)}, u32[]{:S(2)}) copy-start(bf16[1024,2048]{1,0:T(8,128)(2,1)} %param.11) | copy-start | bytes 12582916
  89.9 51.2 %collective-permute-start.6 = (bf16[1024,1024]{1,0:T(8,128)(2,1)}, bf16[1024,1024]{1,0:T(8,128)(2,1)}, u32[]{:S(2)}, u32[]{:S(2)}) collective-permute-start(bf16[1024,1024]{1,0:T(8,128)(2,1)} %get-tuple-element.14.refs_4_), channel_id=1, source_target_pairs={{0,8},{4,12},{8,0},{12,4},{16,24},{20,28},{24,16},{28,20},{1,9},{5... | collective-permute-start | bytes 6291464 | tf_op jit(solution)/shard_map/ppermute | solution.py:17
  95.2 141.8 %collective-permute-start.1 = (bf16[1024,1024]{1,0:T(8,128)(2,1)}, bf16[1024,1024]{1,0:T(8,128)(2,1)}, u32[]{:S(2)}, u32[]{:S(2)}) collective-permute-start(bf16[1024,1024]{1,0:T(8,128)(2,1)} %get-tuple-element.13.refs_4_), channel_id=1, source_target_pairs={{0,8},{4,12},{8,0},{12,4},{16,24},{20,28},{24,16},{28,20},{1,9},{5... | collective-permute-start | bytes 6291464 | tf_op jit(solution)/shard_map/ppermute | solution.py:17
  95.3 153.4 %collective-permute-start.5 = (bf16[1024,1024]{1,0:T(8,128)(2,1)}, bf16[1024,1024]{1,0:T(8,128)(2,1)}, u32[]{:S(2)}, u32[]{:S(2)}) collective-permute-start(bf16[1024,1024]{1,0:T(8,128)(2,1)} %get-tuple-element.14.refs_4_), channel_id=1, source_target_pairs={{0,4},{4,0},{8,12},{12,8},{16,20},{20,16},{24,28},{28,24},{1,5},{5... | collective-permute-start | bytes 6291464 | tf_op jit(solution)/shard_map/ppermute | solution.py:17
  97.8 146.6 %collective-permute-start.20 = (bf16[1024,1024]{1,0:T(8,128)(2,1)}, bf16[1024,1024]{1,0:T(8,128)(2,1)}, u32[]{:S(2)}, u32[]{:S(2)}) collective-permute-start(bf16[1024,1024]{1,0:T(8,128)(2,1)} %get-tuple-element.12.refs_4_), channel_id=1, source_target_pairs={{0,8},{4,12},{8,0},{12,4},{16,24},{20,28},{24,16},{28,20},{1,9},{5... | collective-permute-start | bytes 6291464 | tf_op jit(solution)/shard_map/ppermute | solution.py:17
  100.9 0.6 copy-start.20
  101.5 41.3 %copy-start.22 = (f32[32]{0:T(128)}, f32[32]{0:T(128)S(1)}, u32[]{:S(2)}) copy-start(f32[32]{0:T(128)S(1)} %slice_reduce_fusion.1) | copy-start | bytes 388
  101.5 41.3 %collective-permute-start.10 = (f32[32]{0:T(128)S(1)}, f32[32]{0:T(128)S(1)}, u32[]{:S(2)}, u32[]{:S(2)}) collective-permute-start(f32[32]{0:T(128)S(1)} %slice_reduce_fusion.1), channel_id=1, source_target_pairs={{0,4},{4,0},{8,12},{12,8},{16,20},{20,16},{24,28},{28,24},{1,5},{5... | collective-permute-start | bytes 392 | tf_op jit(solution)/shard_map/ppermute | solution.py:17
  141.1 108.4 %collective-permute-start.7 = (bf16[1024,1024]{1,0:T(8,128)(2,1)}, bf16[1024,1024]{1,0:T(8,128)(2,1)}, u32[]{:S(2)}, u32[]{:S(2)}) collective-permute-start(bf16[1024,1024]{1,0:T(8,128)(2,1)} %collective-permute-done.6.refs_6_), channel_id=1, source_target_pairs={{0,4},{4,0},{8,12},{12,8},{16,20},{20,16},{24,28},{28,24},{1,5},{5... | collective-permute-start | bytes 6291464 | tf_op jit(solution)/shard_map/ppermute | solution.py:17
  143.4 87.6 %collective-permute-start.12 = (f32[32]{0:T(128)S(1)}, f32[32]{0:T(128)S(1)}, u32[]{:S(2)}, u32[]{:S(2)}) collective-permute-start(f32[32]{0:T(128)S(1)} %get-tuple-element.8), channel_id=1, source_target_pairs={{0,8},{4,12},{8,0},{12,4},{16,24},{20,28},{24,16},{28,20},{1,9},{5... | collective-permute-start | bytes 392 | tf_op jit(solution)/shard_map/ppermute | solution.py:17
  145.2 97.9 %copy-start.28 = (f32[32]{0:T(128)S(1)}, f32[32]{0:T(128)}, u32[]{:S(2)}) copy-start(f32[32]{0:T(128)} %get-tuple-element.7) | copy-start | bytes 388
  231.5 3.3 collective-permute-start.14
  232.3 13.5 %copy-start.7 = (f32[32,64,256]{2,1,0:T(8,128)S(1)}, f32[32,64,256]{2,1,0:T(8,128)}, u32[]{:S(2)}) copy-start(f32[32,64,256]{2,1,0:T(8,128)} %param.15) | copy-start | bytes 6291460
  234.9 23.9 %collective-permute-start = (bf16[1024,1024]{1,0:T(8,128)(2,1)}, bf16[1024,1024]{1,0:T(8,128)(2,1)}, u32[]{:S(2)}, u32[]{:S(2)}) collective-permute-start(bf16[1024,1024]{1,0:T(8,128)(2,1)} %get-tuple-element.13.refs_4_), channel_id=1, source_target_pairs={{0,4},{4,0},{8,12},{12,8},{16,20},{20,16},{24,28},{28,24},{1,5},{5... | collective-permute-start | bytes 6291464 | tf_op jit(solution)/shard_map/ppermute | solution.py:17
  237.1 21.8 %collective-permute-start.2 = (bf16[1024,1024]{1,0:T(8,128)(2,1)}, bf16[1024,1024]{1,0:T(8,128)(2,1)}, u32[]{:S(2)}, u32[]{:S(2)}) collective-permute-start(bf16[1024,1024]{1,0:T(8,128)(2,1)} %collective-permute-done.1.refs_6_), channel_id=1, source_target_pairs={{0,4},{4,0},{8,12},{12,8},{16,20},{20,16},{24,28},{28,24},{1,5},{5... | collective-permute-start | bytes 6291464 | tf_op jit(solution)/shard_map/ppermute | solution.py:17
  244.4 76.5 %collective-permute-start.16 = (bf16[1024,1024]{1,0:T(8,128)(2,1)S(1)}, bf16[1024,1024]{1,0:T(8,128)(2,1)}, u32[]{:S(2)}, u32[]{:S(2)}) collective-permute-start(bf16[1024,1024]{1,0:T(8,128)(2,1)S(1)} %get-tuple-element.11.refs_4_), channel_id=1, source_target_pairs={{0,8},{4,12},{8,0},{12,4},{16,24},{20,28},{24,16},{28,20},{1,9},{5... | collective-permute-start | bytes 6291464 | tf_op jit(solution)/shard_map/ppermute | solution.py:17
  248.7 112.9 %collective-permute-start.19 = (bf16[1024,1024]{1,0:T(8,128)(2,1)}, bf16[1024,1024]{1,0:T(8,128)(2,1)}, u32[]{:S(2)}, u32[]{:S(2)}) collective-permute-start(bf16[1024,1024]{1,0:T(8,128)(2,1)} %get-tuple-element.12.refs_4_), channel_id=1, source_target_pairs={{0,4},{4,0},{8,12},{12,8},{16,20},{20,16},{24,28},{28,24},{1,5},{5... | collective-permute-start | bytes 6291464 | tf_op jit(solution)/shard_map/ppermute | solution.py:17
  249.4 112.1 %collective-permute-start.21 = (bf16[1024,1024]{1,0:T(8,128)(2,1)}, bf16[1024,1024]{1,0:T(8,128)(2,1)}, u32[]{:S(2)}, u32[]{:S(2)}) collective-permute-start(bf16[1024,1024]{1,0:T(8,128)(2,1)} %collective-permute-done.20.refs_6_), channel_id=1, source_target_pairs={{0,4},{4,0},{8,12},{12,8},{16,20},{20,16},{24,28},{28,24},{1,5},{5... | collective-permute-start | bytes 6291464 | tf_op jit(solution)/shard_map/ppermute | solution.py:17
  249.5 2.2 copy-start.2
  258.8 63.4 %collective-permute-start.8 = (bf16[512,1024]{1,0:T(8,128)(2,1)S(1)}, bf16[512,1024]{1,0:T(8,128)(2,1)}, u32[]{:S(2)}, u32[]{:S(2)}) collective-permute-start(bf16[512,1024]{1,0:T(8,128)(2,1)S(1)} %shard_map.94), channel_id=1, source_target_pairs={{0,16},{4,20},{8,24},{12,28},{16,0},{20,4},{24,8},{28,12},{1,17},{... | collective-permute-start | bytes 3145736 | tf_op jit(solution)/shard_map/ppermute | solution.py:101
  266.7 82.1 %collective-permute-start.4 = (bf16[512,1024]{1,0:T(8,128)(2,1)}, bf16[512,1024]{1,0:T(8,128)(2,1)}, u32[]{:S(2)}, u32[]{:S(2)}) collective-permute-start(bf16[512,1024]{1,0:T(8,128)(2,1)} %shard_map.92), channel_id=1, source_target_pairs={{0,16},{4,20},{8,24},{12,28},{16,0},{20,4},{24,8},{28,12},{1,17},{... | collective-permute-start | bytes 3145736 | tf_op jit(solution)/shard_map/ppermute | solution.py:101
  320.9 59.8 %collective-permute-start.15 = (bf16[1024,1024]{1,0:T(8,128)(2,1)S(1)}, bf16[1024,1024]{1,0:T(8,128)(2,1)}, u32[]{:S(2)}, u32[]{:S(2)}) collective-permute-start(bf16[1024,1024]{1,0:T(8,128)(2,1)S(1)} %get-tuple-element.11.refs_4_), channel_id=1, source_target_pairs={{0,4},{4,0},{8,12},{12,8},{16,20},{20,16},{24,28},{28,24},{1,5},{5... | collective-permute-start | bytes 6291464 | tf_op jit(solution)/shard_map/ppermute | solution.py:17
  322.2 58.5 %collective-permute-start.17 = (bf16[1024,1024]{1,0:T(8,128)(2,1)}, bf16[1024,1024]{1,0:T(8,128)(2,1)}, u32[]{:S(2)}, u32[]{:S(2)}) collective-permute-start(bf16[1024,1024]{1,0:T(8,128)(2,1)} %collective-permute-done.16.refs_6_), channel_id=1, source_target_pairs={{0,4},{4,0},{8,12},{12,8},{16,20},{20,16},{24,28},{28,24},{1,5},{5... | collective-permute-start | bytes 6291464 | tf_op jit(solution)/shard_map/ppermute | solution.py:17
  351.8 4.0 copy-start.12
  351.8 4.0 copy-start.19
  360.4 27.3 %collective-permute-start.9 = (bf16[32,64,256]{2,1,0:T(8,128)(2,1)S(1)}, bf16[32,64,256]{2,1,0:T(8,128)(2,1)S(1)}, u32[]{:S(2)}, u32[]{:S(2)}) collective-permute-start(bf16[32,64,256]{2,1,0:T(8,128)(2,1)S(1)} %get-tuple-element.33), channel_id=1, source_target_pairs={{0,4},{4,0},{8,12},{12,8},{16,20},{20,16},{24,28},{28,24},{1,5},{5... | collective-permute-start | bytes 3145736 | tf_op jit(solution)/shard_map/ppermute | solution.py:17
  361.5 8.9 %copy-start.3 = (bf16[512,4096]{1,0:T(8,128)(2,1)S(1)}, bf16[512,4096]{1,0:T(8,128)(2,1)}, u32[]{:S(2)}) copy-start(bf16[512,4096]{1,0:T(8,128)(2,1)} %all-gather.6.cloned.1.call-done.refs_0_.refs_1_.refs_2_.refs_3_) | copy-start | bytes 12582916
  377.5 10.2 %copy-start.23 = (f32[32]{0:T(128)S(1)}, f32[32]{0:T(128)}, u32[]{:S(2)}) copy-start(f32[32]{0:T(128)} %get-tuple-element.31) | copy-start | bytes 388
  377.5 10.2 %copy-start.24 = (f32[32]{0:T(128)S(1)}, f32[32]{0:T(128)}, u32[]{:S(2)}) copy-start(f32[32]{0:T(128)} %get-tuple-element.32) | copy-start | bytes 388
  377.5 70.8 %collective-permute-start.22 = (bf16[512,1024]{1,0:T(8,128)(2,1)S(1)}, bf16[512,1024]{1,0:T(8,128)(2,1)S(1)}, u32[]{:S(2)}, u32[]{:S(2)}) collective-permute-start(bf16[512,1024]{1,0:T(8,128)(2,1)S(1)} %shard_map.98), channel_id=1, source_target_pairs={{0,16},{4,20},{8,24},{12,28},{16,0},{20,4},{24,8},{28,12},{1,17},{... | collective-permute-start | bytes 3145736 | tf_op jit(solution)/shard_map/ppermute | solution.py:101
  387.6 83.2 %collective-permute-start.18 = (bf16[512,1024]{1,0:T(8,128)(2,1)S(1)}, bf16[512,1024]{1,0:T(8,128)(2,1)S(1)}, u32[]{:S(2)}, u32[]{:S(2)}) collective-permute-start(bf16[512,1024]{1,0:T(8,128)(2,1)S(1)} %shard_map.96), channel_id=1, source_target_pairs={{0,16},{4,20},{8,24},{12,28},{16,0},{20,4},{24,8},{28,12},{1,17},{... | collective-permute-start | bytes 3145736 | tf_op jit(solution)/shard_map/ppermute | solution.py:101
  388.3 82.8 %collective-permute-start.11 = (bf16[32,64,256]{2,1,0:T(8,128)(2,1)S(1)}, bf16[32,64,256]{2,1,0:T(8,128)(2,1)S(1)}, u32[]{:S(2)}, u32[]{:S(2)}) collective-permute-start(bf16[32,64,256]{2,1,0:T(8,128)(2,1)S(1)} %get-tuple-element.9), channel_id=1, source_target_pairs={{0,8},{4,12},{8,0},{12,4},{16,24},{20,28},{24,16},{28,20},{1,9},{5... | collective-permute-start | bytes 3145736 | tf_op jit(solution)/shard_map/ppermute | solution.py:17
  471.1 0.7 copy-start.25
  471.1 0.7 copy-start.26
  471.1 1.5 copy-start.9
  472.7 13.9 %collective-permute-start.13 = (bf16[8,64,256]{2,1,0:T(8,128)(2,1)}, bf16[8,64,256]{2,1,0:T(8,128)(2,1)}, u32[]{:S(2)}, u32[]{:S(2)}) collective-permute-start(bf16[8,64,256]{2,1,0:T(8,128)(2,1)} %select_convert_fusion.4), channel_id=1, source_target_pairs={{0,16},{4,20},{8,24},{12,28},{16,0},{20,4},{24,8},{28,12},{1,17},{... | collective-permute-start | bytes 786440 | tf_op jit(solution)/shard_map/ppermute | solution.py:17
  478.3 8.3 %copy-start.8 = (bf16[512,2048]{0,1:T(8,128)(2,1)S(1)}, bf16[512,2048]{0,1:T(8,128)(2,1)}, u32[]{:S(2)}) copy-start(bf16[512,2048]{0,1:T(8,128)(2,1)} %copy.39) | copy-start | bytes 6291460
  498.9 8.0 %copy-start.21 = (f32[32]{0:T(128)S(1)}, f32[32]{0:T(128)}, u32[]{:S(2)}) copy-start(f32[32]{0:T(128)} %get-tuple-element.5) | copy-start | bytes 388
  506.9 2.5 copy-start.5
  506.9 2.8 copy-start.10
  506.9 2.8 copy-start.13
  506.9 2.8 copy-start.14
  506.9 2.8 copy-start.15
  506.9 2.8 copy-start.16
  506.9 2.8 copy-start.17
  506.9 2.8 copy-start.18
  506.9 2.8 copy-start.27
  506.9 2.8 copy-start.29
  517.5 2.4 copy-start.1
Sparse Core Ops, SparseCore 0:
  84.4 56.1 all-gather.5
  142.4 52.5 all-gather.3
  486.7 20.0 all-gather.7
